TPU v7x, 256 devices: a whole 4x4x8 slice. The times are simulated.
256 devices in a mesh: depth: 8 (over z_hi, y), lat: 32 (over z_lo, x, core).
Axes of the slice: x: 4, y: 4, z: 8 (z_hi: 2, z_lo: 4; z = z_hi * 4 + z_lo), core: 2. Of those that a mesh axis runs over, the one named last changes fastest.
Arguments:
- down_state: bfloat16 [8, 192, 65536], P('depth', None, 'lat'), may hold values from -6 to 6
- up_state: bfloat16 [8, 192, 65536], P('depth', None, 'lat'), may hold values from -6 to 6
- reflectivity: float32 [8, 65536], P('depth', 'lat'), may hold values from -0.3 to 0.3
- w_down: bfloat16 [8, 32, 2048, 1024], P('depth', 'lat'), may hold values from -0.125 to 0.125
- w_up: bfloat16 [8, 32, 2048, 1024], P('depth', 'lat'), may hold values from -0.125 to 0.125
Outputs:
- down_final: bfloat16 [8, 192, 65536], P('depth', None, 'lat')
- up_final: bfloat16 [8, 192, 65536], P('depth', None, 'lat')
All inputs are finite; a program needn't handle non-finite values.
Results may differ from a plain program's by a relative error of at most 0.0086.
Values may be sent and summed in bfloat16 or wider, within the bound.
No kernel may reach another device: no remote copies, remote signals or barrier semaphores. Data moves between devices by JAX's collectives and lax.ppermute only.
A program may use at most 64 MiB of HBM per device.

v0:
```python
import jax
import jax.numpy as jnp
from jax import lax
from jax.sharding import PartitionSpec as P

BLOCK = 1024
HALO = 512
TICKS = 4


def extended(cells, sides, width):
    for axis, dim in sides:
        count = lax.axis_size(axis)
        ends = count - 1
        head = lax.slice_in_dim(cells, 0, width, axis=dim)
        tail = lax.slice_in_dim(cells, cells.shape[dim] - width, cells.shape[dim], axis=dim)
        cells = jnp.concatenate(
            [
                lax.ppermute(tail, axis, [(i, (i + 1) % count) for i in range(ends)]),
                cells,
                lax.ppermute(head, axis, [((i + 1) % count, i) for i in range(ends)]),
            ],
            axis=dim,
        )
    return cells


def shifted(shard, axis, by):
    size = lax.axis_size(axis)
    pairs = [(i, i + by) for i in range(size) if 0 <= i + by < size]
    return lax.ppermute(shard, axis, pairs)


def windows_of(padded, blocks):
    return jnp.concatenate(
        [
            padded[:, block_index * BLOCK : block_index * BLOCK + BLOCK + 2 * HALO]
            for block_index in range(blocks)
        ],
        axis=0,
    )


def one_tick(going_down, going_up, reflect_row, weights, blocks, at_surface):
    columns = going_down.shape[0]
    down_wide = going_down.astype(jnp.float32)
    up_wide = going_up.astype(jnp.float32)
    mixed_down = ((1.0 + reflect_row) * down_wide - reflect_row * up_wide).astype(jnp.bfloat16)
    mixed_up = ((1.0 - reflect_row) * up_wide + reflect_row * down_wide).astype(jnp.bfloat16)
    stacked = jnp.stack([mixed_down, mixed_up])
    padded = extended(stacked, (("lat", 2),), HALO)
    extrapolated = []
    for member in range(2):
        weight = weights[member]
        zero_rimmed = jnp.pad(stacked[member], ((0, 0), (HALO, HALO)))
        summed = jnp.dot(
            windows_of(zero_rimmed, blocks), weight, preferred_element_type=jnp.float32
        )
        summed = summed.reshape(blocks, columns, BLOCK)
        summed = summed.at[0].add(
            jnp.dot(padded[member][:, :HALO], weight[:HALO], preferred_element_type=jnp.float32)
        )
        summed = summed.at[blocks - 1].add(
            jnp.dot(
                padded[member][:, -HALO:],
                weight[HALO + BLOCK :],
                preferred_element_type=jnp.float32,
            )
        )
        extrapolated.append(
            summed.transpose(1, 0, 2).reshape(columns, blocks * BLOCK).astype(jnp.bfloat16)
        )
    sent_down = shifted(extrapolated[0], "depth", 1)
    sent_up = shifted(extrapolated[1], "depth", -1)
    return (jnp.where(at_surface, -extrapolated[1], sent_down), sent_up)


def on_device(down_state, up_state, reflectivity, w_down, w_up):
    going_down = down_state[0]
    going_up = up_state[0]
    reflect_row = reflectivity[0][None, :]
    weights = (w_down[0, 0], w_up[0, 0])
    at_surface = lax.axis_index("depth") == 0
    blocks = going_down.shape[1] // BLOCK
    for tick_index in range(TICKS):
        going_down, going_up = one_tick(
            going_down, going_up, reflect_row, weights, blocks, at_surface
        )
    return (going_down[None], going_up[None])


def solution(mesh):
    in_specs = (
        P("depth", None, "lat"),
        P("depth", None, "lat"),
        P("depth", "lat"),
        P("depth", "lat", None, None),
        P("depth", "lat", None, None),
    )
    out_specs = (P("depth", None, "lat"), P("depth", None, "lat"))
    return jax.shard_map(
        on_device, mesh=mesh, in_specs=in_specs, out_specs=out_specs, check_vma=False
    )
```

profile of v0, /device:TPU:199, one launch (start us, length us, event | category | flops | bytes accessed | tf_op | source)
XLA Modules:
  0.0 237.4 jit_solution(17332372623569009805)
XLA Ops:
  1.3 1.9 fusion.37
  3.3 3.3 %collective-permute-start = (bf16[2,192,512]{2,1,0:T(8,128)(2,1)S(1)}, bf16[2,192,512]{2,1,0:T(8,128)(2,1)S(1)}, u32[]{:S(2)}, u32[]{:S(2)}) collective-permute-start(bf16[2,192,512]{2,1,0:T(8,128)(2,1)S(1)} %get-tuple-element.218), channel_id=1, source_target_pairs={{0,1},{1,2},{2,3},{3,4},{4,5},{5,6},{6,7},{7,8},{8,9},{9,10},{10,1... | collective-permute-start | bytes 1179656 | tf_op jit(solution)/shard_map/ppermute | solution.py:19
  6.6 1.9 collective-permute-start.1
  15.2 2.6 %collective-permute-done.1 = bf16[2,192,512]{2,1,0:T(8,128)(2,1)S(1)} collective-permute-done((bf16[2,192,512]{2,1,0:T(8,128)(2,1)S(1)}, bf16[2,192,512]{2,1,0:T(8,128)(2,1)S(1)}, u32[]{:S(2)}, u32[]{:S(2)}) %collective-permute-start.1) | collective-permute-done | bytes 393248 | tf_op jit(solution)/shard_map/ppermute | solution.py:21
  19.2 3.2 %collective-permute-start.3 = (bf16[192,2048]{1,0:T(8,128)(2,1)S(1)}, bf16[192,2048]{1,0:T(8,128)(2,1)S(1)}, u32[]{:S(2)}, u32[]{:S(2)}) collective-permute-start(bf16[192,2048]{1,0:T(8,128)(2,1)S(1)} %bitcast.282), channel_id=1, source_target_pairs={{0,32},{32,64},{64,96},{96,128},{128,160},{160,192},{192,224},{1,3... | collective-permute-start | bytes 2359304 | tf_op jit(solution)/shard_map/ppermute | solution.py:31
  23.4 8.1 %collective-permute-start.2 = (bf16[192,2048]{1,0:T(8,128)(2,1)S(1)}, bf16[192,2048]{1,0:T(8,128)(2,1)S(1)}, u32[]{:S(2)}, u32[]{:S(2)}) collective-permute-start(bf16[192,2048]{1,0:T(8,128)(2,1)S(1)} %bitcast.268), channel_id=1, source_target_pairs={{32,0},{64,32},{96,64},{128,96},{160,128},{192,160},{224,192},{33,... | collective-permute-start | bytes 2359304 | tf_op jit(solution)/shard_map/ppermute | solution.py:31
  31.5 30.9 %collective-permute-done.3 = bf16[192,2048]{1,0:T(8,128)(2,1)S(1)} collective-permute-done((bf16[192,2048]{1,0:T(8,128)(2,1)S(1)}, bf16[192,2048]{1,0:T(8,128)(2,1)S(1)}, u32[]{:S(2)}, u32[]{:S(2)}) %collective-permute-start.3) | collective-permute-done | bytes 786464 | tf_op jit(solution)/shard_map/ppermute | solution.py:31
  62.4 2.7 %collective-permute-done.2 = bf16[192,2048]{1,0:T(8,128)(2,1)S(1)} collective-permute-done((bf16[192,2048]{1,0:T(8,128)(2,1)S(1)}, bf16[192,2048]{1,0:T(8,128)(2,1)S(1)}, u32[]{:S(2)}, u32[]{:S(2)}) %collective-permute-start.2) | collective-permute-done | bytes 786464 | tf_op jit(solution)/shard_map/ppermute | solution.py:31
  66.2 2.2 collective-permute-start.4
  68.4 2.6 %collective-permute-start.5 = (bf16[2,192,512]{2,1,0:T(8,128)(2,1)S(1)}, bf16[2,192,512]{2,1,0:T(8,128)(2,1)S(1)}, u32[]{:S(2)}, u32[]{:S(2)}) collective-permute-start(bf16[2,192,512]{2,1,0:T(8,128)(2,1)S(1)} %get-tuple-element.217), channel_id=1, source_target_pairs={{1,0},{2,1},{3,2},{4,3},{5,4},{6,5},{7,6},{8,7},{9,8},{10,9},{11,1... | collective-permute-start | bytes 1179656 | tf_op jit(solution)/shard_map/ppermute | solution.py:21
  73.3 1.8 fusion.4
  75.1 6.7 %collective-permute-done.5 = bf16[2,192,512]{2,1,0:T(8,128)(2,1)S(1)} collective-permute-done((bf16[2,192,512]{2,1,0:T(8,128)(2,1)S(1)}, bf16[2,192,512]{2,1,0:T(8,128)(2,1)S(1)}, u32[]{:S(2)}, u32[]{:S(2)}) %collective-permute-start.5) | collective-permute-done | bytes 393248 | tf_op jit(solution)/shard_map/ppermute | solution.py:21
  83.2 1.9 collective-permute-start.7
  86.1 9.4 %collective-permute-start.6 = (bf16[192,2048]{1,0:T(8,128)(2,1)S(1)}, bf16[192,2048]{1,0:T(8,128)(2,1)S(1)}, u32[]{:S(2)}, u32[]{:S(2)}) collective-permute-start(bf16[192,2048]{1,0:T(8,128)(2,1)S(1)} %bitcast.272), channel_id=1, source_target_pairs={{32,0},{64,32},{96,64},{128,96},{160,128},{192,160},{224,192},{33,... | collective-permute-start | bytes 2359304 | tf_op jit(solution)/shard_map/ppermute | solution.py:31
  95.5 24.0 %collective-permute-done.7 = bf16[192,2048]{1,0:T(8,128)(2,1)S(1)} collective-permute-done((bf16[192,2048]{1,0:T(8,128)(2,1)S(1)}, bf16[192,2048]{1,0:T(8,128)(2,1)S(1)}, u32[]{:S(2)}, u32[]{:S(2)}) %collective-permute-start.7) | collective-permute-done | bytes 786464 | tf_op jit(solution)/shard_map/ppermute | solution.py:31
  119.5 2.7 %collective-permute-done.6 = bf16[192,2048]{1,0:T(8,128)(2,1)S(1)} collective-permute-done((bf16[192,2048]{1,0:T(8,128)(2,1)S(1)}, bf16[192,2048]{1,0:T(8,128)(2,1)S(1)}, u32[]{:S(2)}, u32[]{:S(2)}) %collective-permute-start.6) | collective-permute-done | bytes 786464 | tf_op jit(solution)/shard_map/ppermute | solution.py:31
  123.3 1.9 collective-permute-start.8
  125.2 2.4 %collective-permute-start.9 = (bf16[2,192,512]{2,1,0:T(8,128)(2,1)S(1)}, bf16[2,192,512]{2,1,0:T(8,128)(2,1)S(1)}, u32[]{:S(2)}, u32[]{:S(2)}) collective-permute-start(bf16[2,192,512]{2,1,0:T(8,128)(2,1)S(1)} %get-tuple-element.215), channel_id=1, source_target_pairs={{1,0},{2,1},{3,2},{4,3},{5,4},{6,5},{7,6},{8,7},{9,8},{10,9},{11,1... | collective-permute-start | bytes 1179656 | tf_op jit(solution)/shard_map/ppermute | solution.py:21
  129.7 1.8 fusion.2
  131.5 9.2 %collective-permute-done.9 = bf16[2,192,512]{2,1,0:T(8,128)(2,1)S(1)} collective-permute-done((bf16[2,192,512]{2,1,0:T(8,128)(2,1)S(1)}, bf16[2,192,512]{2,1,0:T(8,128)(2,1)S(1)}, u32[]{:S(2)}, u32[]{:S(2)}) %collective-permute-start.9) | collective-permute-done | bytes 393248 | tf_op jit(solution)/shard_map/ppermute | solution.py:21
  142.1 1.9 collective-permute-start.11
  145.0 9.6 %collective-permute-start.10 = (bf16[192,2048]{1,0:T(8,128)(2,1)S(1)}, bf16[192,2048]{1,0:T(8,128)(2,1)S(1)}, u32[]{:S(2)}, u32[]{:S(2)}) collective-permute-start(bf16[192,2048]{1,0:T(8,128)(2,1)S(1)} %bitcast.270), channel_id=1, source_target_pairs={{32,0},{64,32},{96,64},{128,96},{160,128},{192,160},{224,192},{33,... | collective-permute-start | bytes 2359304 | tf_op jit(solution)/shard_map/ppermute | solution.py:31
  154.6 18.4 %collective-permute-done.11 = bf16[192,2048]{1,0:T(8,128)(2,1)S(1)} collective-permute-done((bf16[192,2048]{1,0:T(8,128)(2,1)S(1)}, bf16[192,2048]{1,0:T(8,128)(2,1)S(1)}, u32[]{:S(2)}, u32[]{:S(2)}) %collective-permute-start.11) | collective-permute-done | bytes 786464 | tf_op jit(solution)/shard_map/ppermute | solution.py:31
  173.1 2.8 %collective-permute-done.10 = bf16[192,2048]{1,0:T(8,128)(2,1)S(1)} collective-permute-done((bf16[192,2048]{1,0:T(8,128)(2,1)S(1)}, bf16[192,2048]{1,0:T(8,128)(2,1)S(1)}, u32[]{:S(2)}, u32[]{:S(2)}) %collective-permute-start.10) | collective-permute-done | bytes 786464 | tf_op jit(solution)/shard_map/ppermute | solution.py:31
  177.0 1.9 collective-permute-start.12
  178.9 2.4 %collective-permute-start.13 = (bf16[2,192,512]{2,1,0:T(8,128)(2,1)S(1)}, bf16[2,192,512]{2,1,0:T(8,128)(2,1)S(1)}, u32[]{:S(2)}, u32[]{:S(2)}) collective-permute-start(bf16[2,192,512]{2,1,0:T(8,128)(2,1)S(1)} %get-tuple-element.213), channel_id=1, source_target_pairs={{1,0},{2,1},{3,2},{4,3},{5,4},{6,5},{7,6},{8,7},{9,8},{10,9},{11,1... | collective-permute-start | bytes 1179656 | tf_op jit(solution)/shard_map/ppermute | solution.py:21
  183.3 1.8 fusion.8
  185.1 9.2 %collective-permute-done.13 = bf16[2,192,512]{2,1,0:T(8,128)(2,1)S(1)} collective-permute-done((bf16[2,192,512]{2,1,0:T(8,128)(2,1)S(1)}, bf16[2,192,512]{2,1,0:T(8,128)(2,1)S(1)}, u32[]{:S(2)}, u32[]{:S(2)}) %collective-permute-start.13) | collective-permute-done | bytes 393248 | tf_op jit(solution)/shard_map/ppermute | solution.py:21
  195.7 7.4 %collective-permute-start.15 = (bf16[192,2048]{1,0:T(8,128)(2,1)S(1)}, bf16[192,2048]{1,0:T(8,128)(2,1)S(1)}, u32[]{:S(2)}, u32[]{:S(2)}) collective-permute-start(bf16[192,2048]{1,0:T(8,128)(2,1)S(1)} %bitcast.266), channel_id=1, source_target_pairs={{32,0},{64,32},{96,64},{128,96},{160,128},{192,160},{224,192},{33,... | collective-permute-start | bytes 2359304 | tf_op jit(solution)/shard_map/ppermute | solution.py:31
  204.2 1.9 collective-permute-start.14
  206.1 18.3 %collective-permute-done.15 = bf16[192,2048]{1,0:T(8,128)(2,1)S(1)} collective-permute-done((bf16[192,2048]{1,0:T(8,128)(2,1)S(1)}, bf16[192,2048]{1,0:T(8,128)(2,1)S(1)}, u32[]{:S(2)}, u32[]{:S(2)}) %collective-permute-start.15) | collective-permute-done | bytes 786464 | tf_op jit(solution)/shard_map/ppermute | solution.py:31
  224.4 11.2 %collective-permute-done.14 = bf16[192,2048]{1,0:T(8,128)(2,1)S(1)} collective-permute-done((bf16[192,2048]{1,0:T(8,128)(2,1)S(1)}, bf16[192,2048]{1,0:T(8,128)(2,1)S(1)}, u32[]{:S(2)}, u32[]{:S(2)}) %collective-permute-start.14) | collective-permute-done | bytes 786464 | tf_op jit(solution)/shard_map/ppermute | solution.py:31
  (89 shorter events, 28.0 us)
Async XLA Ops:
  3.2 5.3 %copy-start.4 = (bf16[1,192,2048]{2,1,0:T(8,128)(2,1)S(1)}, bf16[1,192,2048]{2,1,0:T(8,128)(2,1)}, u32[]{:S(2)}) copy-start(bf16[1,192,2048]{2,1,0:T(8,128)(2,1)} %param.37) | copy-start | bytes 2359300
  3.3 5.3 %copy-start.5 = (bf16[1,192,2048]{2,1,0:T(8,128)(2,1)S(1)}, bf16[1,192,2048]{2,1,0:T(8,128)(2,1)}, u32[]{:S(2)}) copy-start(bf16[1,192,2048]{2,1,0:T(8,128)(2,1)} %param.38) | copy-start | bytes 2359300
  3.3 5.3 %copy-start.6 = (f32[1,2048]{1,0:T(1,128)S(1)}, f32[1,2048]{1,0:T(1,128)}, u32[]{:S(2)}) copy-start(f32[1,2048]{1,0:T(1,128)} %param.39) | copy-start | bytes 24580
  3.3 11.9 %collective-permute-start = (bf16[2,192,512]{2,1,0:T(8,128)(2,1)S(1)}, bf16[2,192,512]{2,1,0:T(8,128)(2,1)S(1)}, u32[]{:S(2)}, u32[]{:S(2)}) collective-permute-start(bf16[2,192,512]{2,1,0:T(8,128)(2,1)S(1)} %get-tuple-element.218), channel_id=1, source_target_pairs={{0,1},{1,2},{2,3},{3,4},{4,5},{5,6},{6,7},{7,8},{8,9},{9,10},{10,1... | collective-permute-start | bytes 1179656 | tf_op jit(solution)/shard_map/ppermute | solution.py:19
  6.6 11.2 %collective-permute-start.1 = (bf16[2,192,512]{2,1,0:T(8,128)(2,1)S(1)}, bf16[2,192,512]{2,1,0:T(8,128)(2,1)S(1)}, u32[]{:S(2)}, u32[]{:S(2)}) collective-permute-start(bf16[2,192,512]{2,1,0:T(8,128)(2,1)S(1)} %get-tuple-element.219), channel_id=1, source_target_pairs={{1,0},{2,1},{3,2},{4,3},{5,4},{6,5},{7,6},{8,7},{9,8},{10,9},{11,1... | collective-permute-start | bytes 1179656 | tf_op jit(solution)/shard_map/ppermute | solution.py:21
  9.1 2.2 copy-start.2
  11.3 2.2 copy-start
  19.2 43.2 %collective-permute-start.3 = (bf16[192,2048]{1,0:T(8,128)(2,1)S(1)}, bf16[192,2048]{1,0:T(8,128)(2,1)S(1)}, u32[]{:S(2)}, u32[]{:S(2)}) collective-permute-start(bf16[192,2048]{1,0:T(8,128)(2,1)S(1)} %bitcast.282), channel_id=1, source_target_pairs={{0,32},{32,64},{64,96},{96,128},{128,160},{160,192},{192,224},{1,3... | collective-permute-start | bytes 2359304 | tf_op jit(solution)/shard_map/ppermute | solution.py:31
  23.4 41.7 %collective-permute-start.2 = (bf16[192,2048]{1,0:T(8,128)(2,1)S(1)}, bf16[192,2048]{1,0:T(8,128)(2,1)S(1)}, u32[]{:S(2)}, u32[]{:S(2)}) collective-permute-start(bf16[192,2048]{1,0:T(8,128)(2,1)S(1)} %bitcast.268), channel_id=1, source_target_pairs={{32,0},{64,32},{96,64},{128,96},{160,128},{192,160},{224,192},{33,... | collective-permute-start | bytes 2359304 | tf_op jit(solution)/shard_map/ppermute | solution.py:31
  66.1 5.0 %copy-start.3 = (bf16[1,1,2048,1024]{3,2,1,0:T(8,128)(2,1)S(1)}, bf16[1,1,2048,1024]{3,2,1,0:T(8,128)(2,1)}, u32[]{:S(2)}) copy-start(bf16[1,1,2048,1024]{3,2,1,0:T(8,128)(2,1)} %param.40) | copy-start | bytes 12582916
  66.2 8.9 %collective-permute-start.4 = (bf16[2,192,512]{2,1,0:T(8,128)(2,1)S(1)}, bf16[2,192,512]{2,1,0:T(8,128)(2,1)S(1)}, u32[]{:S(2)}, u32[]{:S(2)}) collective-permute-start(bf16[2,192,512]{2,1,0:T(8,128)(2,1)S(1)} %get-tuple-element.216), channel_id=1, source_target_pairs={{0,1},{1,2},{2,3},{3,4},{4,5},{5,6},{6,7},{7,8},{8,9},{9,10},{10,1... | collective-permute-start | bytes 1179656 | tf_op jit(solution)/shard_map/ppermute | solution.py:19
  68.4 13.4 %collective-permute-start.5 = (bf16[2,192,512]{2,1,0:T(8,128)(2,1)S(1)}, bf16[2,192,512]{2,1,0:T(8,128)(2,1)S(1)}, u32[]{:S(2)}, u32[]{:S(2)}) collective-permute-start(bf16[2,192,512]{2,1,0:T(8,128)(2,1)S(1)} %get-tuple-element.217), channel_id=1, source_target_pairs={{1,0},{2,1},{3,2},{4,3},{5,4},{6,5},{7,6},{8,7},{9,8},{10,9},{11,1... | collective-permute-start | bytes 1179656 | tf_op jit(solution)/shard_map/ppermute | solution.py:21
  71.1 2.2 copy-start.1
  83.2 36.3 %collective-permute-start.7 = (bf16[192,2048]{1,0:T(8,128)(2,1)S(1)}, bf16[192,2048]{1,0:T(8,128)(2,1)S(1)}, u32[]{:S(2)}, u32[]{:S(2)}) collective-permute-start(bf16[192,2048]{1,0:T(8,128)(2,1)S(1)} %bitcast.284), channel_id=1, source_target_pairs={{0,32},{32,64},{64,96},{96,128},{128,160},{160,192},{192,224},{1,3... | collective-permute-start | bytes 2359304 | tf_op jit(solution)/shard_map/ppermute | solution.py:31
  86.1 36.1 %collective-permute-start.6 = (bf16[192,2048]{1,0:T(8,128)(2,1)S(1)}, bf16[192,2048]{1,0:T(8,128)(2,1)S(1)}, u32[]{:S(2)}, u32[]{:S(2)}) collective-permute-start(bf16[192,2048]{1,0:T(8,128)(2,1)S(1)} %bitcast.272), channel_id=1, source_target_pairs={{32,0},{64,32},{96,64},{128,96},{160,128},{192,160},{224,192},{33,... | collective-permute-start | bytes 2359304 | tf_op jit(solution)/shard_map/ppermute | solution.py:31
  123.3 8.2 %collective-permute-start.8 = (bf16[2,192,512]{2,1,0:T(8,128)(2,1)S(1)}, bf16[2,192,512]{2,1,0:T(8,128)(2,1)S(1)}, u32[]{:S(2)}, u32[]{:S(2)}) collective-permute-start(bf16[2,192,512]{2,1,0:T(8,128)(2,1)S(1)} %get-tuple-element.214), channel_id=1, source_target_pairs={{0,1},{1,2},{2,3},{3,4},{4,5},{5,6},{6,7},{7,8},{8,9},{9,10},{10,1... | collective-permute-start | bytes 1179656 | tf_op jit(solution)/shard_map/ppermute | solution.py:19
  125.2 15.5 %collective-permute-start.9 = (bf16[2,192,512]{2,1,0:T(8,128)(2,1)S(1)}, bf16[2,192,512]{2,1,0:T(8,128)(2,1)S(1)}, u32[]{:S(2)}, u32[]{:S(2)}) collective-permute-start(bf16[2,192,512]{2,1,0:T(8,128)(2,1)S(1)} %get-tuple-element.215), channel_id=1, source_target_pairs={{1,0},{2,1},{3,2},{4,3},{5,4},{6,5},{7,6},{8,7},{9,8},{10,9},{11,1... | collective-permute-start | bytes 1179656 | tf_op jit(solution)/shard_map/ppermute | solution.py:21
  142.1 31.0 %collective-permute-start.11 = (bf16[192,2048]{1,0:T(8,128)(2,1)S(1)}, bf16[192,2048]{1,0:T(8,128)(2,1)S(1)}, u32[]{:S(2)}, u32[]{:S(2)}) collective-permute-start(bf16[192,2048]{1,0:T(8,128)(2,1)S(1)} %bitcast.285), channel_id=1, source_target_pairs={{0,32},{32,64},{64,96},{96,128},{128,160},{160,192},{192,224},{1,3... | collective-permute-start | bytes 2359304 | tf_op jit(solution)/shard_map/ppermute | solution.py:31
  145.0 30.8 %collective-permute-start.10 = (bf16[192,2048]{1,0:T(8,128)(2,1)S(1)}, bf16[192,2048]{1,0:T(8,128)(2,1)S(1)}, u32[]{:S(2)}, u32[]{:S(2)}) collective-permute-start(bf16[192,2048]{1,0:T(8,128)(2,1)S(1)} %bitcast.270), channel_id=1, source_target_pairs={{32,0},{64,32},{96,64},{128,96},{160,128},{192,160},{224,192},{33,... | collective-permute-start | bytes 2359304 | tf_op jit(solution)/shard_map/ppermute | solution.py:31
  177.0 8.2 %collective-permute-start.12 = (bf16[2,192,512]{2,1,0:T(8,128)(2,1)S(1)}, bf16[2,192,512]{2,1,0:T(8,128)(2,1)S(1)}, u32[]{:S(2)}, u32[]{:S(2)}) collective-permute-start(bf16[2,192,512]{2,1,0:T(8,128)(2,1)S(1)} %get-tuple-element.212), channel_id=1, source_target_pairs={{0,1},{1,2},{2,3},{3,4},{4,5},{5,6},{6,7},{7,8},{8,9},{9,10},{10,1... | collective-permute-start | bytes 1179656 | tf_op jit(solution)/shard_map/ppermute | solution.py:19
  178.9 15.4 %collective-permute-start.13 = (bf16[2,192,512]{2,1,0:T(8,128)(2,1)S(1)}, bf16[2,192,512]{2,1,0:T(8,128)(2,1)S(1)}, u32[]{:S(2)}, u32[]{:S(2)}) collective-permute-start(bf16[2,192,512]{2,1,0:T(8,128)(2,1)S(1)} %get-tuple-element.213), channel_id=1, source_target_pairs={{1,0},{2,1},{3,2},{4,3},{5,4},{6,5},{7,6},{8,7},{9,8},{10,9},{11,1... | collective-permute-start | bytes 1179656 | tf_op jit(solution)/shard_map/ppermute | solution.py:21
  195.7 28.7 %collective-permute-start.15 = (bf16[192,2048]{1,0:T(8,128)(2,1)S(1)}, bf16[192,2048]{1,0:T(8,128)(2,1)S(1)}, u32[]{:S(2)}, u32[]{:S(2)}) collective-permute-start(bf16[192,2048]{1,0:T(8,128)(2,1)S(1)} %bitcast.266), channel_id=1, source_target_pairs={{32,0},{64,32},{96,64},{128,96},{160,128},{192,160},{224,192},{33,... | collective-permute-start | bytes 2359304 | tf_op jit(solution)/shard_map/ppermute | solution.py:31
  204.2 31.4 %collective-permute-start.14 = (bf16[192,2048]{1,0:T(8,128)(2,1)S(1)}, bf16[192,2048]{1,0:T(8,128)(2,1)S(1)}, u32[]{:S(2)}, u32[]{:S(2)}) collective-permute-start(bf16[192,2048]{1,0:T(8,128)(2,1)S(1)} %bitcast.286), channel_id=1, source_target_pairs={{0,32},{32,64},{64,96},{96,128},{128,160},{160,192},{192,224},{1,3... | collective-permute-start | bytes 2359304 | tf_op jit(solution)/shard_map/ppermute | solution.py:31
where the time goes:
time: 238 us; the launch traced here: 237 us
  waiting for transfers between devices  139 us (58%)
  starting transfers between devices  62.1 us (26%)
  matrix products  20.8 us (9%)
  other arithmetic  8.87 us (4%)
  local copies, waits for them, and re-layouts  5.64 us (2%)
    ppermute x8, waiting for transfers between devices, shifted(): return lax.ppermute(shard, axis, pairs)  111 us
    ppermute x8, starting transfers between devices, shifted(): return lax.ppermute(shard, axis, pairs)  43.5 us
    ppermute x4, waiting for transfers between devices, extended(): lax.ppermute(head, axis, [((i + 1) % count, i) for i in range(ends)])  27.7 us
    dot_general x8, matrix products, one_tick(): jnp.dot(windows_of(zero_rimmed, blocks), weight, preferred_element_type=j...  14.3 us
    ppermute x4, starting transfers between devices, extended(): lax.ppermute(head, axis, [((i + 1) % count, i) for i in range(ends)])  9.32 us
    ppermute x4, starting transfers between devices, extended(): lax.ppermute(tail, axis, [(i, (i + 1) % count) for i in range(ends)])  9.28 us
  transfers between devices with their start and end apart: 16, of which 12 were waited for; matrix products, arithmetic and copies ran while one was open for 8% of the time, Pallas kernels for 0%

commit v1 on v0

v1 whole, which is shorter than its diff:
```python
import functools

import jax
import jax.numpy as jnp
from jax import lax
from jax.experimental import pallas as pl
from jax.experimental.pallas import tpu as pltpu
from jax.sharding import PartitionSpec as P

BLOCK = 1024
HALO = 512
TICKS = 4
CHUNKS = ((192, 80),)

SPLIT_EDGE = True
VMEM = pl.BlockSpec(memory_space=pltpu.VMEM)
SMEM = pl.BlockSpec(memory_space=pltpu.SMEM)


def swap(*pairs):
    return [q for a, b in pairs for q in ((a, b), (b, a))]


INNER = swap((1, 2), (5, 6))
FIRST_DIRECT = INNER + swap((3, 4))
FIRST_STEP = INNER + [(3, 0), (4, 7)]
FIRST_FORWARD = [(0, 4), (7, 3)]
SECOND = swap((0, 1), (2, 3), (4, 5), (6, 7))


def call(body, outs, ins, name):
    many = isinstance(outs, (tuple, list))
    return pl.pallas_call(
        body,
        out_shape=outs,
        in_specs=[SMEM] + [VMEM] * (len(ins) - 1),
        out_specs=tuple(VMEM for _ in outs) if many else VMEM,
        compiler_params=pltpu.CompilerParams(vmem_limit_bytes=20 * 1024 * 1024),
        cost_estimate=pl.CostEstimate(flops=1, transcendentals=0, bytes_accessed=1),
        name=name,
    )(*ins)


def store_mixed(scal, sign, first, second, reflect, m_ref, e1_ref, e2_ref, rows):
    rho = reflect * jnp.where(scal[0] == 1, 1.0, -1.0)
    first = first.astype(jnp.float32)
    second = second.astype(jnp.float32)
    mixed = (
        (1.0 + rho) * first - (rho * sign) * second,
        ((1.0 - rho) * sign) * second + rho * first,
    )
    size = mixed[0].shape[1]
    for f in range(2):
        value = mixed[f].astype(jnp.bfloat16)
        m_ref[f, rows, :] = value
        head = value[:, :HALO]
        tail = value[:, size - HALO :]
        even = scal[2] == 0
        e1_ref[f, rows, :] = jnp.where(even, tail, head)
        e2_ref[f, rows, :] = jnp.where(even, head, tail)


def mix_start(scal, down, up, reflect, m_ref, e1_ref, e2_ref):
    odd = scal[0] == 1
    first = jnp.where(odd, down[...], up[...])
    second = jnp.where(odd, up[...], down[...])
    store_mixed(scal, 1.0, first, second, reflect[...], m_ref, e1_ref, e2_ref, slice(None))


def second_parts(scal, own_direct, own_step, got_direct, got_step, got_forward):
    level = scal[1]
    direct = jnp.where(level == 0, own_direct[...], got_direct[...])
    step = jnp.where(
        level == 0,
        own_step[...],
        jnp.where(
            (level == 3) | (level == 4),
            got_forward[...],
            jnp.where(level == 7, jnp.zeros_like(got_step[...]), got_step[...]),
        ),
    )
    return direct, step


def mix_next(scal, first, own_direct, own_step, got_direct, got_step, got_forward, reflect, m_ref, e1_ref, e2_ref):
    sign = jnp.where(scal[1] == 0, -1.0, 1.0)
    direct, step = second_parts(scal, own_direct, own_step, got_direct, got_step, got_forward)
    cut = direct.shape[0]
    rows = first.shape[0]
    value = first[...]
    store_mixed(scal, sign, value[:cut], direct, reflect[...], m_ref, e1_ref, e2_ref, pl.ds(0, cut))
    store_mixed(scal, sign, value[cut:], step, reflect[...], m_ref, e1_ref, e2_ref, pl.ds(cut, rows - cut))


def load_weights(scal, order, w_down, w_up, out, sems):
    del order

    def both(*sources):
        copies = [pltpu.make_async_copy(w.at[0, 0], out.at[f], sems.at[f]) for f, w in enumerate(sources)]
        for copy in copies:
            copy.start()
        for copy in copies:
            copy.wait()

    @pl.when(scal[0] == 1)
    def _():
        both(w_down, w_up)

    @pl.when(scal[0] == 0)
    def _():
        both(w_up, w_down)


def weights_by_role(scal, order, w_down, w_up):
    return pl.pallas_call(
        load_weights,
        out_shape=jax.ShapeDtypeStruct((2, 2 * BLOCK, BLOCK), jnp.bfloat16),
        in_specs=[SMEM] + [pl.BlockSpec(memory_space=pl.ANY)] * 3,
        out_specs=VMEM,
        scratch_shapes=[pltpu.SemaphoreType.DMA((2,))],
        compiler_params=pltpu.CompilerParams(vmem_limit_bytes=20 * 1024 * 1024),
        cost_estimate=pl.CostEstimate(flops=1, transcendentals=0, bytes_accessed=1),
        name="weights",
    )(scal, order, w_down, w_up)


def body_dots(scal, m_ref, w_ref, acc_ref):
    for f in range(2):
        left = jnp.concatenate([m_ref[f, :, :BLOCK], m_ref[f, :, BLOCK:]], axis=0)
        acc_ref[f] = jnp.dot(
            left, w_ref[f, HALO : HALO + BLOCK, :], preferred_element_type=jnp.float32
        )


def edge_dots(scal, m_ref, h1_ref, h2_ref, acc_ref, w_ref, *outs, fields):
    even = scal[2] == 0
    for field, parts in zip(fields, outs if len(fields) == 1 else (outs[:2], outs[2:])):
        parts = outs if len(fields) == 1 else parts
        h1 = h1_ref[field]
        h2 = h2_ref[field]
        from_left = jnp.where(even, h2, h1)
        from_right = jnp.where(even, h1, h2)
        columns = h1.shape[0]
        low = jnp.concatenate([from_left, m_ref[field, :, HALO:BLOCK]], axis=0)
        high = jnp.concatenate([m_ref[field, :, BLOCK : BLOCK + HALO], from_right], axis=0)
        summed = (
            acc_ref[field]
            + jnp.dot(low, w_ref[field, :HALO, :], preferred_element_type=jnp.float32)
            + jnp.dot(high, w_ref[field, HALO + BLOCK :, :], preferred_element_type=jnp.float32)
        ).astype(jnp.bfloat16)
        start = 0
        for out in parts:
            rows = out.shape[0]
            out[:, :BLOCK] = summed[start : start + rows]
            out[:, BLOCK:] = summed[columns + start : columns + start + rows]
            start += rows


def finish(scal, *refs):
    down_ref, up_ref = refs[-2:]
    sign = jnp.where(scal[1] == 0, -1.0, 1.0).astype(jnp.bfloat16)
    odd = scal[0] == 1
    start = 0
    for c in range(len(CHUNKS)):
        first, *rest = refs[6 * c : 6 * c + 6]
        for part in second_parts(scal, *rest):
            rows = part.shape[0]
            one = first[pl.ds(start - sum(n for n, _ in CHUNKS[:c]), rows), :]
            two = part * sign
            down_ref[0, pl.ds(start, rows), :] = jnp.where(odd, one, two)
            up_ref[0, pl.ds(start, rows), :] = jnp.where(odd, two, one)
            start += rows


def on_device(down_state, up_state, reflectivity, w_down, w_up):
    level = lax.axis_index("depth")
    tile = lax.axis_index("lat")
    tiles = lax.axis_size("lat")
    scal = jnp.stack([level % 2, level, tile % 2]).astype(jnp.int32)
    inside = swap(*[(i, i + 1) for i in range(0, tiles, 2)])
    outside = swap(*[(i, i + 1) for i in range(1, tiles - 1, 2)])
    wide = down_state.shape[2]
    bf = lambda *s: jax.ShapeDtypeStruct(s, jnp.bfloat16)
    state = []
    start = 0
    for n, _ in CHUNKS:
        state.append((down_state[0, start : start + n], up_state[0, start : start + n]))
        start += n
    weights = None
    for tick in range(TICKS):
        for c, (n, k) in enumerate(CHUNKS):
            m, e1, e2 = call(
                mix_start if tick == 0 else mix_next,
                (bf(2, n, wide), bf(2, n, HALO), bf(2, n, HALO)),
                (scal, *state[c], reflectivity),
                "mix",
            )
            h2 = lax.ppermute(e2, "lat", outside)
            h1 = lax.ppermute(e1, "lat", inside)
            if weights is None:
                weights = weights_by_role(scal, m, w_down, w_up)
            acc = call(
                body_dots,
                jax.ShapeDtypeStruct((2, 2 * n, BLOCK), jnp.float32),
                (scal, m, weights),
                "body",
            )
            if SPLIT_EDGE:
                own = call(
                    functools.partial(edge_dots, fields=(0,)),
                    (bf(n - k, wide), bf(k, wide)),
                    (scal, m, h1, h2, acc, weights),
                    "edge0",
                )
                (other,) = call(
                    functools.partial(edge_dots, fields=(1,)),
                    (bf(n, wide),),
                    (scal, m, h1, h2, acc, weights),
                    "edge1",
                )
            else:
                *own, other = call(
                    functools.partial(edge_dots, fields=(0, 1)),
                    (bf(n - k, wide), bf(k, wide), bf(n, wide)),
                    (scal, m, h1, h2, acc, weights),
                    "edges",
                )
            got_direct = lax.ppermute(own[0], "depth", FIRST_DIRECT)
            got_step = lax.ppermute(own[1], "depth", FIRST_STEP)
            first = lax.ppermute(other, "depth", SECOND)
            got_forward = lax.ppermute(got_step, "depth", FIRST_FORWARD)
            state[c] = (first, *own, got_direct, got_step, got_forward)
    total = sum(n for n, _ in CHUNKS)
    return call(
        finish,
        (bf(1, total, wide), bf(1, total, wide)),
        (scal, *[x for s in state for x in s]),
        "finish",
    )


def solution(mesh):
    in_specs = (
        P("depth", None, "lat"),
        P("depth", None, "lat"),
        P("depth", "lat"),
        P("depth", "lat", None, None),
        P("depth", "lat", None, None),
    )
    out_specs = (P("depth", None, "lat"), P("depth", None, "lat"))
    return jax.shard_map(
        on_device, mesh=mesh, in_specs=in_specs, out_specs=out_specs, check_vma=False
    )
```

time: 238 us -> 196 us (0.82)
  the two profiles are of different devices: /device:TPU:199 before, /device:TPU:57 now
where the time goes in v1:
time: 196 us; the launch traced here: 193 us
  waiting for transfers between devices  93.1 us (48%)
  starting transfers between devices  61.4 us (31%)
  Pallas kernels  29.6 us (15%)
  local copies, waits for them, and re-layouts  7.34 us (4%)
    ppermute x4, waiting for transfers between devices, on_device(): got_direct = lax.ppermute(own[0], 'depth', FIRST_DIRECT)  78.3 us
    ppermute x4, starting transfers between devices, on_device(): got_direct = lax.ppermute(own[0], 'depth', FIRST_DIRECT)  31.9 us
    pallas_call x17, Pallas kernels, call(): pl.pallas_call(body, out_shape=outs, in_specs=[SMEM] + [VMEM] * (len(ins)...  28.5 us
    ppermute x4, starting transfers between devices, on_device(): h2 = lax.ppermute(e2, 'lat', outside)  12.7 us
    ppermute x4, waiting for transfers between devices, on_device(): h2 = lax.ppermute(e2, 'lat', outside)  11.4 us
    unnamed x12, local copies, waits for them, and re-layouts  7.34 us
    ppermute x4, starting transfers between devices, on_device(): got_step = lax.ppermute(own[1], 'depth', FIRST_STEP)  6.63 us
    ppermute x4, starting transfers between devices, on_device(): got_forward = lax.ppermute(got_step, 'depth', FIRST_FORWARD)  5.17 us
  transfers between devices with their start and end apart: 24, of which 11 were waited for; matrix products, arithmetic and copies ran while one was open for 0% of the time, Pallas kernels for 9%

profile of v1, /device:TPU:57, one launch (start us, length us, event | category | flops | bytes accessed | tf_op | source)
XLA Modules:
  0.0 192.6 jit_solution(1032617587107957200)
XLA Ops:
  5.7 3.0 %collective-permute-start.1 = (bf16[2,192,512]{2,1,0:T(8,128)(2,1)S(1)}, bf16[2,192,512]{2,1,0:T(8,128)(2,1)S(1)}, u32[]{:S(2)}, u32[]{:S(2)}) collective-permute-start(bf16[2,192,512]{2,1,0:T(8,128)(2,1)S(1)} %get-tuple-element.24), channel_id=1, source_target_pairs={{1,2},{2,1},{3,4},{4,3},{5,6},{6,5},{7,8},{8,7},{9,10},{10,9},{11,... | collective-permute-start | bytes 1179656 | tf_op jit(solution)/shard_map/ppermute | solution.py:198
  8.8 2.2 %copy-done = bf16[1,1,2048,1024]{3,2,1,0:T(8,128)(2,1)S(1)} copy-done((bf16[1,1,2048,1024]{3,2,1,0:T(8,128)(2,1)S(1)}, bf16[1,1,2048,1024]{3,2,1,0:T(8,128)(2,1)}, u32[]{:S(2)}) %copy-start) | copy-done | bytes 4194328
  10.9 2.2 %copy-done.1 = bf16[1,1,2048,1024]{3,2,1,0:T(8,128)(2,1)S(1)} copy-done((bf16[1,1,2048,1024]{3,2,1,0:T(8,128)(2,1)S(1)}, bf16[1,1,2048,1024]{3,2,1,0:T(8,128)(2,1)}, u32[]{:S(2)}) %copy-start.1) | copy-done | bytes 4194328
  14.3 2.3 %body.4.acc_ref = f32[2,384,1024]{2,1,0:T(8,128)S(1)} custom-call(s32[3]{0:T(128)S(1)} %pad_add_fusion.scal, bf16[2,192,2048]{2,1,0:T(8,128)(2,1)S(1)} %get-tuple-element.22.order.m_ref, bf16[2,2048,1024]{2,1,0:T(8,128)(2,1)S(1)} %weights.1.w_ref), custom_call_target="tpu_custom_call" | custom-call | flops 1 | bytes 1 | tf_op jit(solution)/shard_map/body/pallas_call | solution.py:33
  16.6 1.5 edge1.4
  20.3 2.7 %collective-permute-start.4 = (bf16[80,2048]{1,0:T(8,128)(2,1)S(1)}, bf16[80,2048]{1,0:T(8,128)(2,1)S(1)}, u32[]{:S(2)}, u32[]{:S(2)}) collective-permute-start(bf16[80,2048]{1,0:T(8,128)(2,1)S(1)} %get-tuple-element.26.own_step), channel_id=1, source_target_pairs={{32,64},{64,32},{160,192},{192,160},{96,0},{128,224},{33,65},{65,3... | collective-permute-start | bytes 983048 | tf_op jit(solution)/shard_map/ppermute | solution.py:229
  23.0 9.5 %collective-permute-start.3 = (bf16[112,2048]{1,0:T(8,128)(2,1)S(1)}, bf16[112,2048]{1,0:T(8,128)(2,1)S(1)}, u32[]{:S(2)}, u32[]{:S(2)}) collective-permute-start(bf16[112,2048]{1,0:T(8,128)(2,1)S(1)} %get-tuple-element.25.own_direct), channel_id=1, source_target_pairs={{32,64},{64,32},{160,192},{192,160},{96,128},{128,96},{33,65},{65,... | collective-permute-start | bytes 1376264 | tf_op jit(solution)/shard_map/ppermute | solution.py:228
  33.8 17.8 %collective-permute-done.3.got_direct = bf16[112,2048]{1,0:T(8,128)(2,1)S(1)} collective-permute-done((bf16[112,2048]{1,0:T(8,128)(2,1)S(1)}, bf16[112,2048]{1,0:T(8,128)(2,1)S(1)}, u32[]{:S(2)}, u32[]{:S(2)}) %collective-permute-start.3) | collective-permute-done | bytes 458784 | tf_op jit(solution)/shard_map/ppermute | solution.py:228
  51.6 2.4 %collective-permute-done.5.got_forward = bf16[80,2048]{1,0:T(8,128)(2,1)S(1)} collective-permute-done((bf16[80,2048]{1,0:T(8,128)(2,1)S(1)}, bf16[80,2048]{1,0:T(8,128)(2,1)S(1)}, u32[]{:S(2)}, u32[]{:S(2)}) %collective-permute-start.5) | collective-permute-done | bytes 327712 | tf_op jit(solution)/shard_map/ppermute | solution.py:231
  55.3 1.6 collective-permute-start.6
  56.8 3.3 %collective-permute-start.7 = (bf16[2,192,512]{2,1,0:T(8,128)(2,1)S(1)}, bf16[2,192,512]{2,1,0:T(8,128)(2,1)S(1)}, u32[]{:S(2)}, u32[]{:S(2)}) collective-permute-start(bf16[2,192,512]{2,1,0:T(8,128)(2,1)S(1)} %get-tuple-element.29), channel_id=1, source_target_pairs={{1,2},{2,1},{3,4},{4,3},{5,6},{6,5},{7,8},{8,7},{9,10},{10,9},{11,... | collective-permute-start | bytes 1179656 | tf_op jit(solution)/shard_map/ppermute | solution.py:198
  60.2 2.3 %body.5.acc_ref = f32[2,384,1024]{2,1,0:T(8,128)S(1)} custom-call(s32[3]{0:T(128)S(1)} %pad_add_fusion.scal, bf16[2,192,2048]{2,1,0:T(8,128)(2,1)S(1)} %get-tuple-element.27.m_ref, bf16[2,2048,1024]{2,1,0:T(8,128)(2,1)S(1)} %weights.1.w_ref), custom_call_target="tpu_custom_call" | custom-call | flops 1 | bytes 1 | tf_op jit(solution)/shard_map/body/pallas_call | solution.py:33
  62.5 3.7 %collective-permute-done.7.h2_ref = bf16[2,192,512]{2,1,0:T(8,128)(2,1)S(1)} collective-permute-done((bf16[2,192,512]{2,1,0:T(8,128)(2,1)S(1)}, bf16[2,192,512]{2,1,0:T(8,128)(2,1)S(1)}, u32[]{:S(2)}, u32[]{:S(2)}) %collective-permute-start.7) | collective-permute-done | bytes 393248 | tf_op jit(solution)/shard_map/ppermute | solution.py:198
  66.2 1.5 edge1.5
  67.8 1.5 edge0.5
  70.7 7.7 %collective-permute-start.9 = (bf16[112,2048]{1,0:T(8,128)(2,1)S(1)}, bf16[112,2048]{1,0:T(8,128)(2,1)S(1)}, u32[]{:S(2)}, u32[]{:S(2)}) collective-permute-start(bf16[112,2048]{1,0:T(8,128)(2,1)S(1)} %get-tuple-element.30.own_direct), channel_id=1, source_target_pairs={{32,64},{64,32},{160,192},{192,160},{96,128},{128,96},{33,65},{65,... | collective-permute-start | bytes 1376264 | tf_op jit(solution)/shard_map/ppermute | solution.py:228
  79.7 20.6 %collective-permute-done.9.got_direct = bf16[112,2048]{1,0:T(8,128)(2,1)S(1)} collective-permute-done((bf16[112,2048]{1,0:T(8,128)(2,1)S(1)}, bf16[112,2048]{1,0:T(8,128)(2,1)S(1)}, u32[]{:S(2)}, u32[]{:S(2)}) %collective-permute-start.9) | collective-permute-done | bytes 458784 | tf_op jit(solution)/shard_map/ppermute | solution.py:228
  102.8 3.3 %collective-permute-start.13 = (bf16[2,192,512]{2,1,0:T(8,128)(2,1)S(1)}, bf16[2,192,512]{2,1,0:T(8,128)(2,1)S(1)}, u32[]{:S(2)}, u32[]{:S(2)}) collective-permute-start(bf16[2,192,512]{2,1,0:T(8,128)(2,1)S(1)} %get-tuple-element.34), channel_id=1, source_target_pairs={{1,2},{2,1},{3,4},{4,3},{5,6},{6,5},{7,8},{8,7},{9,10},{10,9},{11,... | collective-permute-start | bytes 1179656 | tf_op jit(solution)/shard_map/ppermute | solution.py:198
  106.0 2.3 %body.6.acc_ref = f32[2,384,1024]{2,1,0:T(8,128)S(1)} custom-call(s32[3]{0:T(128)S(1)} %pad_add_fusion.scal, bf16[2,192,2048]{2,1,0:T(8,128)(2,1)S(1)} %get-tuple-element.32.m_ref, bf16[2,2048,1024]{2,1,0:T(8,128)(2,1)S(1)} %weights.1.w_ref), custom_call_target="tpu_custom_call" | custom-call | flops 1 | bytes 1 | tf_op jit(solution)/shard_map/body/pallas_call | solution.py:33
  108.4 3.7 %collective-permute-done.13.h2_ref = bf16[2,192,512]{2,1,0:T(8,128)(2,1)S(1)} collective-permute-done((bf16[2,192,512]{2,1,0:T(8,128)(2,1)S(1)}, bf16[2,192,512]{2,1,0:T(8,128)(2,1)S(1)}, u32[]{:S(2)}, u32[]{:S(2)}) %collective-permute-start.13) | collective-permute-done | bytes 393248 | tf_op jit(solution)/shard_map/ppermute | solution.py:198
  112.1 1.5 edge1.6
  113.8 1.5 edge0.6
  116.6 7.7 %collective-permute-start.15 = (bf16[112,2048]{1,0:T(8,128)(2,1)S(1)}, bf16[112,2048]{1,0:T(8,128)(2,1)S(1)}, u32[]{:S(2)}, u32[]{:S(2)}) collective-permute-start(bf16[112,2048]{1,0:T(8,128)(2,1)S(1)} %get-tuple-element.35.own_direct), channel_id=1, source_target_pairs={{32,64},{64,32},{160,192},{192,160},{96,128},{128,96},{33,65},{65,... | collective-permute-start | bytes 1376264 | tf_op jit(solution)/shard_map/ppermute | solution.py:228
  125.7 20.3 %collective-permute-done.15.got_direct = bf16[112,2048]{1,0:T(8,128)(2,1)S(1)} collective-permute-done((bf16[112,2048]{1,0:T(8,128)(2,1)S(1)}, bf16[112,2048]{1,0:T(8,128)(2,1)S(1)}, u32[]{:S(2)}, u32[]{:S(2)}) %collective-permute-start.15) | collective-permute-done | bytes 458784 | tf_op jit(solution)/shard_map/ppermute | solution.py:228
  148.8 3.0 %collective-permute-start.19 = (bf16[2,192,512]{2,1,0:T(8,128)(2,1)S(1)}, bf16[2,192,512]{2,1,0:T(8,128)(2,1)S(1)}, u32[]{:S(2)}, u32[]{:S(2)}) collective-permute-start(bf16[2,192,512]{2,1,0:T(8,128)(2,1)S(1)} %get-tuple-element.39), channel_id=1, source_target_pairs={{1,2},{2,1},{3,4},{4,3},{5,6},{6,5},{7,8},{8,7},{9,10},{10,9},{11,... | collective-permute-start | bytes 1179656 | tf_op jit(solution)/shard_map/ppermute | solution.py:198
  151.9 2.3 %body.7.acc_ref = f32[2,384,1024]{2,1,0:T(8,128)S(1)} custom-call(s32[3]{0:T(128)S(1)} %pad_add_fusion.scal, bf16[2,192,2048]{2,1,0:T(8,128)(2,1)S(1)} %get-tuple-element.37.m_ref, bf16[2,2048,1024]{2,1,0:T(8,128)(2,1)S(1)} %weights.1.w_ref), custom_call_target="tpu_custom_call" | custom-call | flops 1 | bytes 1 | tf_op jit(solution)/shard_map/body/pallas_call | solution.py:33
  154.2 4.0 %collective-permute-done.19.h2_ref = bf16[2,192,512]{2,1,0:T(8,128)(2,1)S(1)} collective-permute-done((bf16[2,192,512]{2,1,0:T(8,128)(2,1)S(1)}, bf16[2,192,512]{2,1,0:T(8,128)(2,1)S(1)}, u32[]{:S(2)}, u32[]{:S(2)}) %collective-permute-start.19) | collective-permute-done | bytes 393248 | tf_op jit(solution)/shard_map/ppermute | solution.py:198
  158.2 1.5 edge1.7
  159.8 1.5 edge0.7
  162.7 6.9 %collective-permute-start.21 = (bf16[112,2048]{1,0:T(8,128)(2,1)S(1)}, bf16[112,2048]{1,0:T(8,128)(2,1)S(1)}, u32[]{:S(2)}, u32[]{:S(2)}) collective-permute-start(bf16[112,2048]{1,0:T(8,128)(2,1)S(1)} %get-tuple-element.40.refs_1_), channel_id=1, source_target_pairs={{32,64},{64,32},{160,192},{192,160},{96,128},{128,96},{33,65},{65,... | collective-permute-start | bytes 1376264 | tf_op jit(solution)/shard_map/ppermute | solution.py:228
  170.9 19.7 %collective-permute-done.21.refs_3_ = bf16[112,2048]{1,0:T(8,128)(2,1)S(1)} collective-permute-done((bf16[112,2048]{1,0:T(8,128)(2,1)S(1)}, bf16[112,2048]{1,0:T(8,128)(2,1)S(1)}, u32[]{:S(2)}, u32[]{:S(2)}) %collective-permute-start.21) | collective-permute-done | bytes 458784 | tf_op jit(solution)/shard_map/ppermute | solution.py:228
  190.7 1.9 finish.1
  (47 shorter events, 24.4 us)
Async XLA Ops:
  0.7 1.1 copy-start.2
  1.9 1.1 copy-start.3
  3.0 0.7 copy-start.4
  5.0 11.7 %collective-permute-start = (bf16[2,192,512]{2,1,0:T(8,128)(2,1)S(1)}, bf16[2,192,512]{2,1,0:T(8,128)(2,1)S(1)}, u32[]{:S(2)}, u32[]{:S(2)}) collective-permute-start(bf16[2,192,512]{2,1,0:T(8,128)(2,1)S(1)} %get-tuple-element.23), channel_id=1, source_target_pairs={{0,1},{1,0},{2,3},{3,2},{4,5},{5,4},{6,7},{7,6},{8,9},{9,8},{10,11... | collective-permute-start | bytes 1179656 | tf_op jit(solution)/shard_map/ppermute | solution.py:199
  5.7 10.9 %collective-permute-start.1 = (bf16[2,192,512]{2,1,0:T(8,128)(2,1)S(1)}, bf16[2,192,512]{2,1,0:T(8,128)(2,1)S(1)}, u32[]{:S(2)}, u32[]{:S(2)}) collective-permute-start(bf16[2,192,512]{2,1,0:T(8,128)(2,1)S(1)} %get-tuple-element.24), channel_id=1, source_target_pairs={{1,2},{2,1},{3,4},{4,3},{5,6},{6,5},{7,8},{8,7},{9,10},{10,9},{11,... | collective-permute-start | bytes 1179656 | tf_op jit(solution)/shard_map/ppermute | solution.py:198
  8.8 2.2 %copy-start = (bf16[1,1,2048,1024]{3,2,1,0:T(8,128)(2,1)S(1)}, bf16[1,1,2048,1024]{3,2,1,0:T(8,128)(2,1)}, u32[]{:S(2)}) copy-start(bf16[1,1,2048,1024]{3,2,1,0:T(8,128)(2,1)} %w_down.1) | copy-start | bytes 12582916
  10.9 2.2 %copy-start.1 = (bf16[1,1,2048,1024]{3,2,1,0:T(8,128)(2,1)S(1)}, bf16[1,1,2048,1024]{3,2,1,0:T(8,128)(2,1)}, u32[]{:S(2)}) copy-start(bf16[1,1,2048,1024]{3,2,1,0:T(8,128)(2,1)} %w_up.1) | copy-start | bytes 12582916
  18.2 35.8 %copy-start.5 = (f32[1,2048]{1,0:T(1,128)S(1)}, f32[1,2048]{1,0:T(1,128)}, u32[]{:S(2)}) copy-start(f32[1,2048]{1,0:T(1,128)} %reflect.7) | copy-start | bytes 24580
  18.2 35.8 %collective-permute-start.2 = (bf16[192,2048]{1,0:T(8,128)(2,1)S(1)}, bf16[192,2048]{1,0:T(8,128)(2,1)S(1)}, u32[]{:S(2)}, u32[]{:S(2)}) collective-permute-start(bf16[192,2048]{1,0:T(8,128)(2,1)S(1)} %edge1.4), channel_id=1, source_target_pairs={{0,32},{32,0},{64,96},{96,64},{128,160},{160,128},{192,224},{224,1... | collective-permute-start | bytes 2359304 | tf_op jit(solution)/shard_map/ppermute | solution.py:230
  20.3 12.3 %collective-permute-start.4 = (bf16[80,2048]{1,0:T(8,128)(2,1)S(1)}, bf16[80,2048]{1,0:T(8,128)(2,1)S(1)}, u32[]{:S(2)}, u32[]{:S(2)}) collective-permute-start(bf16[80,2048]{1,0:T(8,128)(2,1)S(1)} %get-tuple-element.26.own_step), channel_id=1, source_target_pairs={{32,64},{64,32},{160,192},{192,160},{96,0},{128,224},{33,65},{65,3... | collective-permute-start | bytes 983048 | tf_op jit(solution)/shard_map/ppermute | solution.py:229
  23.0 28.6 %collective-permute-start.3 = (bf16[112,2048]{1,0:T(8,128)(2,1)S(1)}, bf16[112,2048]{1,0:T(8,128)(2,1)S(1)}, u32[]{:S(2)}, u32[]{:S(2)}) collective-permute-start(bf16[112,2048]{1,0:T(8,128)(2,1)S(1)} %get-tuple-element.25.own_direct), channel_id=1, source_target_pairs={{32,64},{64,32},{160,192},{192,160},{96,128},{128,96},{33,65},{65,... | collective-permute-start | bytes 1376264 | tf_op jit(solution)/shard_map/ppermute | solution.py:228
  32.5 21.5 %collective-permute-start.5 = (bf16[80,2048]{1,0:T(8,128)(2,1)S(1)}, bf16[80,2048]{1,0:T(8,128)(2,1)S(1)}, u32[]{:S(2)}, u32[]{:S(2)}) collective-permute-start(bf16[80,2048]{1,0:T(8,128)(2,1)S(1)} %collective-permute-done.4.got_step), channel_id=1, source_target_pairs={{0,128},{224,96},{1,129},{225,97},{2,130},{226,98},{3,131},{227,99... | collective-permute-start | bytes 983048 | tf_op jit(solution)/shard_map/ppermute | solution.py:231
  55.3 7.2 %collective-permute-start.6 = (bf16[2,192,512]{2,1,0:T(8,128)(2,1)S(1)}, bf16[2,192,512]{2,1,0:T(8,128)(2,1)S(1)}, u32[]{:S(2)}, u32[]{:S(2)}) collective-permute-start(bf16[2,192,512]{2,1,0:T(8,128)(2,1)S(1)} %get-tuple-element.28), channel_id=1, source_target_pairs={{0,1},{1,0},{2,3},{3,2},{4,5},{5,4},{6,7},{7,6},{8,9},{9,8},{10,11... | collective-permute-start | bytes 1179656 | tf_op jit(solution)/shard_map/ppermute | solution.py:199
  56.8 9.4 %collective-permute-start.7 = (bf16[2,192,512]{2,1,0:T(8,128)(2,1)S(1)}, bf16[2,192,512]{2,1,0:T(8,128)(2,1)S(1)}, u32[]{:S(2)}, u32[]{:S(2)}) collective-permute-start(bf16[2,192,512]{2,1,0:T(8,128)(2,1)S(1)} %get-tuple-element.29), channel_id=1, source_target_pairs={{1,2},{2,1},{3,4},{4,3},{5,6},{6,5},{7,8},{8,7},{9,10},{10,9},{11,... | collective-permute-start | bytes 1179656 | tf_op jit(solution)/shard_map/ppermute | solution.py:198
  67.7 33.1 %collective-permute-start.8 = (bf16[192,2048]{1,0:T(8,128)(2,1)S(1)}, bf16[192,2048]{1,0:T(8,128)(2,1)S(1)}, u32[]{:S(2)}, u32[]{:S(2)}) collective-permute-start(bf16[192,2048]{1,0:T(8,128)(2,1)S(1)} %edge1.5), channel_id=1, source_target_pairs={{0,32},{32,0},{64,96},{96,64},{128,160},{160,128},{192,224},{224,1... | collective-permute-start | bytes 2359304 | tf_op jit(solution)/shard_map/ppermute | solution.py:230
  69.4 9.0 %collective-permute-start.10 = (bf16[80,2048]{1,0:T(8,128)(2,1)S(1)}, bf16[80,2048]{1,0:T(8,128)(2,1)S(1)}, u32[]{:S(2)}, u32[]{:S(2)}) collective-permute-start(bf16[80,2048]{1,0:T(8,128)(2,1)S(1)} %get-tuple-element.31.own_step), channel_id=1, source_target_pairs={{32,64},{64,32},{160,192},{192,160},{96,0},{128,224},{33,65},{65,3... | collective-permute-start | bytes 983048 | tf_op jit(solution)/shard_map/ppermute | solution.py:229
  70.7 29.6 %collective-permute-start.9 = (bf16[112,2048]{1,0:T(8,128)(2,1)S(1)}, bf16[112,2048]{1,0:T(8,128)(2,1)S(1)}, u32[]{:S(2)}, u32[]{:S(2)}) collective-permute-start(bf16[112,2048]{1,0:T(8,128)(2,1)S(1)} %get-tuple-element.30.own_direct), channel_id=1, source_target_pairs={{32,64},{64,32},{160,192},{192,160},{96,128},{128,96},{33,65},{65,... | collective-permute-start | bytes 1376264 | tf_op jit(solution)/shard_map/ppermute | solution.py:228
  78.4 22.4 %collective-permute-start.11 = (bf16[80,2048]{1,0:T(8,128)(2,1)S(1)}, bf16[80,2048]{1,0:T(8,128)(2,1)S(1)}, u32[]{:S(2)}, u32[]{:S(2)}) collective-permute-start(bf16[80,2048]{1,0:T(8,128)(2,1)S(1)} %collective-permute-done.10.got_step), channel_id=1, source_target_pairs={{0,128},{224,96},{1,129},{225,97},{2,130},{226,98},{3,131},{227,99... | collective-permute-start | bytes 983048 | tf_op jit(solution)/shard_map/ppermute | solution.py:231
  102.1 6.3 %collective-permute-start.12 = (bf16[2,192,512]{2,1,0:T(8,128)(2,1)S(1)}, bf16[2,192,512]{2,1,0:T(8,128)(2,1)S(1)}, u32[]{:S(2)}, u32[]{:S(2)}) collective-permute-start(bf16[2,192,512]{2,1,0:T(8,128)(2,1)S(1)} %get-tuple-element.33), channel_id=1, source_target_pairs={{0,1},{1,0},{2,3},{3,2},{4,5},{5,4},{6,7},{7,6},{8,9},{9,8},{10,11... | collective-permute-start | bytes 1179656 | tf_op jit(solution)/shard_map/ppermute | solution.py:199
  102.8 9.4 %collective-permute-start.13 = (bf16[2,192,512]{2,1,0:T(8,128)(2,1)S(1)}, bf16[2,192,512]{2,1,0:T(8,128)(2,1)S(1)}, u32[]{:S(2)}, u32[]{:S(2)}) collective-permute-start(bf16[2,192,512]{2,1,0:T(8,128)(2,1)S(1)} %get-tuple-element.34), channel_id=1, source_target_pairs={{1,2},{2,1},{3,4},{4,3},{5,6},{6,5},{7,8},{8,7},{9,10},{10,9},{11,... | collective-permute-start | bytes 1179656 | tf_op jit(solution)/shard_map/ppermute | solution.py:198
  113.7 32.6 %collective-permute-start.14 = (bf16[192,2048]{1,0:T(8,128)(2,1)S(1)}, bf16[192,2048]{1,0:T(8,128)(2,1)S(1)}, u32[]{:S(2)}, u32[]{:S(2)}) collective-permute-start(bf16[192,2048]{1,0:T(8,128)(2,1)S(1)} %edge1.6), channel_id=1, source_target_pairs={{0,32},{32,0},{64,96},{96,64},{128,160},{160,128},{192,224},{224,1... | collective-permute-start | bytes 2359304 | tf_op jit(solution)/shard_map/ppermute | solution.py:230
  115.3 9.1 %collective-permute-start.16 = (bf16[80,2048]{1,0:T(8,128)(2,1)S(1)}, bf16[80,2048]{1,0:T(8,128)(2,1)S(1)}, u32[]{:S(2)}, u32[]{:S(2)}) collective-permute-start(bf16[80,2048]{1,0:T(8,128)(2,1)S(1)} %get-tuple-element.36.own_step), channel_id=1, source_target_pairs={{32,64},{64,32},{160,192},{192,160},{96,0},{128,224},{33,65},{65,3... | collective-permute-start | bytes 983048 | tf_op jit(solution)/shard_map/ppermute | solution.py:229
  116.6 29.3 %collective-permute-start.15 = (bf16[112,2048]{1,0:T(8,128)(2,1)S(1)}, bf16[112,2048]{1,0:T(8,128)(2,1)S(1)}, u32[]{:S(2)}, u32[]{:S(2)}) collective-permute-start(bf16[112,2048]{1,0:T(8,128)(2,1)S(1)} %get-tuple-element.35.own_direct), channel_id=1, source_target_pairs={{32,64},{64,32},{160,192},{192,160},{96,128},{128,96},{33,65},{65,... | collective-permute-start | bytes 1376264 | tf_op jit(solution)/shard_map/ppermute | solution.py:228
  124.4 21.9 %collective-permute-start.17 = (bf16[80,2048]{1,0:T(8,128)(2,1)S(1)}, bf16[80,2048]{1,0:T(8,128)(2,1)S(1)}, u32[]{:S(2)}, u32[]{:S(2)}) collective-permute-start(bf16[80,2048]{1,0:T(8,128)(2,1)S(1)} %collective-permute-done.16.got_step), channel_id=1, source_target_pairs={{0,128},{224,96},{1,129},{225,97},{2,130},{226,98},{3,131},{227,99... | collective-permute-start | bytes 983048 | tf_op jit(solution)/shard_map/ppermute | solution.py:231
  147.5 6.7 %collective-permute-start.18 = (bf16[2,192,512]{2,1,0:T(8,128)(2,1)S(1)}, bf16[2,192,512]{2,1,0:T(8,128)(2,1)S(1)}, u32[]{:S(2)}, u32[]{:S(2)}) collective-permute-start(bf16[2,192,512]{2,1,0:T(8,128)(2,1)S(1)} %get-tuple-element.38), channel_id=1, source_target_pairs={{0,1},{1,0},{2,3},{3,2},{4,5},{5,4},{6,7},{7,6},{8,9},{9,8},{10,11... | collective-permute-start | bytes 1179656 | tf_op jit(solution)/shard_map/ppermute | solution.py:199
  148.8 9.4 %collective-permute-start.19 = (bf16[2,192,512]{2,1,0:T(8,128)(2,1)S(1)}, bf16[2,192,512]{2,1,0:T(8,128)(2,1)S(1)}, u32[]{:S(2)}, u32[]{:S(2)}) collective-permute-start(bf16[2,192,512]{2,1,0:T(8,128)(2,1)S(1)} %get-tuple-element.39), channel_id=1, source_target_pairs={{1,2},{2,1},{3,4},{4,3},{5,6},{6,5},{7,8},{8,7},{9,10},{10,9},{11,... | collective-permute-start | bytes 1179656 | tf_op jit(solution)/shard_map/ppermute | solution.py:198
  159.7 31.0 %collective-permute-start.20 = (bf16[192,2048]{1,0:T(8,128)(2,1)S(1)}, bf16[192,2048]{1,0:T(8,128)(2,1)S(1)}, u32[]{:S(2)}, u32[]{:S(2)}) collective-permute-start(bf16[192,2048]{1,0:T(8,128)(2,1)S(1)} %edge1.7), channel_id=1, source_target_pairs={{0,32},{32,0},{64,96},{96,64},{128,160},{160,128},{192,224},{224,1... | collective-permute-start | bytes 2359304 | tf_op jit(solution)/shard_map/ppermute | solution.py:230
  161.4 8.2 %collective-permute-start.22 = (bf16[80,2048]{1,0:T(8,128)(2,1)S(1)}, bf16[80,2048]{1,0:T(8,128)(2,1)S(1)}, u32[]{:S(2)}, u32[]{:S(2)}) collective-permute-start(bf16[80,2048]{1,0:T(8,128)(2,1)S(1)} %get-tuple-element.41.refs_2_), channel_id=1, source_target_pairs={{32,64},{64,32},{160,192},{192,160},{96,0},{128,224},{33,65},{65,3... | collective-permute-start | bytes 983048 | tf_op jit(solution)/shard_map/ppermute | solution.py:229
  162.7 27.9 %collective-permute-start.21 = (bf16[112,2048]{1,0:T(8,128)(2,1)S(1)}, bf16[112,2048]{1,0:T(8,128)(2,1)S(1)}, u32[]{:S(2)}, u32[]{:S(2)}) collective-permute-start(bf16[112,2048]{1,0:T(8,128)(2,1)S(1)} %get-tuple-element.40.refs_1_), channel_id=1, source_target_pairs={{32,64},{64,32},{160,192},{192,160},{96,128},{128,96},{33,65},{65,... | collective-permute-start | bytes 1376264 | tf_op jit(solution)/shard_map/ppermute | solution.py:228
  169.6 21.1 %collective-permute-start.23 = (bf16[80,2048]{1,0:T(8,128)(2,1)S(1)}, bf16[80,2048]{1,0:T(8,128)(2,1)S(1)}, u32[]{:S(2)}, u32[]{:S(2)}) collective-permute-start(bf16[80,2048]{1,0:T(8,128)(2,1)S(1)} %collective-permute-done.22.refs_4_), channel_id=1, source_target_pairs={{0,128},{224,96},{1,129},{225,97},{2,130},{226,98},{3,131},{227,99... | collective-permute-start | bytes 983048 | tf_op jit(solution)/shard_map/ppermute | solution.py:231

commit v2 on v0

v2 whole, which is shorter than its diff:
```python
import functools

import jax
import jax.numpy as jnp
from jax import lax
from jax.experimental import pallas as pl
from jax.experimental.pallas import tpu as pltpu
from jax.sharding import PartitionSpec as P

BLOCK = 1024
HALO = 512
TICKS = 4
STEP_ROWS = 64
HFLIP = False
GRANT = 20 * 1024 * 1024
HINT = 10_000_000_000

VMEM = pl.BlockSpec(memory_space=pltpu.VMEM)
SMEM = pl.BlockSpec(memory_space=pltpu.SMEM)
HBM = pl.BlockSpec(memory_space=pltpu.HBM)


def swap(*pairs):
    return [q for a, b in pairs for q in ((a, b), (b, a))]


INNER = swap((1, 2), (5, 6))
FIRST_DIRECT = INNER + swap((3, 4))
FIRST_STEP = INNER + [(3, 0), (4, 7)]
FIRST_FORWARD = [(0, 4), (7, 3)]
SECOND = swap((0, 1), (2, 3), (4, 5), (6, 7))


def bf(*shape):
    return jax.ShapeDtypeStruct(shape, jnp.bfloat16)


def f32(*shape):
    return jax.ShapeDtypeStruct(shape, jnp.float32)


def call(body, outs, ins, name, specs=None, scratch=(), out_specs=None, aliases=None):
    return pl.pallas_call(
        body,
        out_shape=tuple(outs),
        in_specs=[SMEM] + (specs or [VMEM] * (len(ins) - 1)),
        out_specs=out_specs or tuple(VMEM for _ in outs),
        scratch_shapes=scratch,
        input_output_aliases=aliases or {},
        compiler_params=pltpu.CompilerParams(vmem_limit_bytes=GRANT),
        cost_estimate=pl.CostEstimate(flops=HINT, transcendentals=0, bytes_accessed=1),
        name=name,
    )(*ins)


def mixed(rho, sign, first, second):
    first = first.astype(jnp.float32)
    second = second.astype(jnp.float32)
    return (
        ((1.0 + rho) * first - (rho * sign) * second).astype(jnp.bfloat16),
        (((1.0 - rho) * sign) * second + rho * first).astype(jnp.bfloat16),
    )


def rho_of(scal, reflect):
    return reflect * jnp.where(scal[0] == 1, 1.0, -1.0)


def sign_of(scal):
    return jnp.where(scal[1] == 0, -1.0, 1.0)


def second_parts(scal, own_direct, own_step, got_direct, got_step, got_forward, cut=slice(None)):
    level = scal[1]
    direct = jnp.where(level == 0, own_direct[:, cut], got_direct[:, cut])
    step = jnp.where((level == 3) | (level == 4), got_forward[:, cut], got_step[:, cut])
    step = jnp.where(level == 7, jnp.zeros_like(step), step)
    return direct, jnp.where(level == 0, own_step[:, cut], step)


def ends_next(scal, first, *refs):
    second = refs[:5]
    reflect, e1_ref, e2_ref = refs[5:]
    size = first.shape[1]
    rho = rho_of(scal, reflect[...])
    sign = sign_of(scal)
    for cut in (slice(0, HALO), slice(size - HALO, size)):
        goes_first = (scal[2] == 0) == (cut.start > 0)
        start = 0
        for part in second_parts(scal, *second, cut=cut):
            rows = pl.ds(start, part.shape[0])
            pair = mixed(rho[:, cut], sign, first[rows, cut], part)

            @pl.when(goes_first)
            def _():
                for f in range(2):
                    e1_ref[f, rows, :] = pair[f]

            @pl.when(jnp.logical_not(goes_first))
            def _():
                for f in range(2):
                    e2_ref[f, rows, :] = pair[f]

            start += part.shape[0]


def ends_start(scal, down, up, reflect, e1_ref, e2_ref, ends_ref, r_ref, sems):
    odd = scal[0] == 1
    even_tile = scal[2] == 0
    size = down.shape[2]
    cuts = (slice(0, HALO), slice(size - HALO, size))
    copies = [pltpu.make_async_copy(reflect, r_ref, sems.at[4])]
    for i, state in enumerate((down, up)):
        for j, cut in enumerate(cuts):
            source = state.at[0, :, pl.ds(cut.start, HALO)]
            copies.append(pltpu.make_async_copy(source, ends_ref.at[i, j], sems.at[2 * i + j]))
    for copy in copies:
        copy.start()
    for copy in copies:
        copy.wait()
    rho = rho_of(scal, r_ref[...])
    for j, cut in enumerate(cuts):
        one, two = ends_ref[0, j], ends_ref[1, j]
        pair = mixed(rho[:, cut], 1.0, jnp.where(odd, one, two), jnp.where(odd, two, one))
        goes_first = even_tile == (j == 1)

        @pl.when(goes_first)
        def _():
            for f in range(2):
                e1_ref[f] = pair[f]

        @pl.when(jnp.logical_not(goes_first))
        def _():
            for f in range(2):
                e2_ref[f] = pair[f]


def dot(left, right):
    return jnp.dot(left, right, preferred_element_type=jnp.float32)


def inner_dots(m_ref, w_ref, acc_ref, f):
    columns = m_ref.shape[1]
    left = jnp.concatenate([m_ref[f, :, :BLOCK], m_ref[f, :, BLOCK:]], axis=0)
    both = dot(left, w_ref[f, HALO : HALO + BLOCK, :])
    acc_ref[f, :columns] = both[:columns] + dot(m_ref[f, :, BLOCK : BLOCK + HALO], w_ref[f, HALO + BLOCK :, :])
    acc_ref[f, columns:] = both[columns:] + dot(m_ref[f, :, HALO:BLOCK], w_ref[f, :HALO, :])


def body_start(scal, down, up, reflect, w_down, w_up, acc_ref, w_ref, m_ref, sems):
    odd = scal[0] == 1

    def copies(*sources):
        return [pltpu.make_async_copy(w.at[0, 0], w_ref.at[f], sems.at[f]) for f, w in enumerate(sources)]

    @pl.when(odd)
    def _():
        for copy in copies(w_down, w_up):
            copy.start()

    @pl.when(jnp.logical_not(odd))
    def _():
        for copy in copies(w_up, w_down):
            copy.start()

    one, two = down[0], up[0]
    pair = mixed(rho_of(scal, reflect[...]), 1.0, jnp.where(odd, one, two), jnp.where(odd, two, one))
    for f in range(2):
        m_ref[f] = pair[f]
    for f, copy in enumerate(copies(w_down, w_up)):
        copy.wait()
        inner_dots(m_ref, w_ref, acc_ref, f)


def body_next(scal, first, *refs):
    reflect, w_ref, acc_ref, m_ref = refs[5:]
    rho = rho_of(scal, reflect[...])
    start = 0
    for part in second_parts(scal, *refs[:5]):
        rows = pl.ds(start, part.shape[0])
        pair = mixed(rho, sign_of(scal), first[rows, :], part)
        for f in range(2):
            m_ref[f, rows, :] = pair[f]
        start += part.shape[0]
    for f in range(2):
        inner_dots(m_ref, w_ref, acc_ref, f)


def halo_dots(scal, h1_ref, h2_ref, acc_ref, w_ref, *outs):
    even = scal[2] == 0
    for f, parts in ((0, outs[:2]), (1, outs[2:])):
        h1 = h1_ref[f]
        h2 = h2_ref[f]
        columns = h1.shape[0]
        left = acc_ref[f, :columns] + dot(jnp.where(even, h2, h1), w_ref[f, :HALO, :])
        right = acc_ref[f, columns:] + dot(jnp.where(even, h1, h2), w_ref[f, HALO + BLOCK :, :])
        start = 0
        for out in parts:
            rows = out.shape[0]
            out[:, :BLOCK] = left[start : start + rows].astype(jnp.bfloat16)
            out[:, BLOCK:] = right[start : start + rows].astype(jnp.bfloat16)
            start += rows


def finish(scal, first, *refs):
    down_ref, up_ref = refs[-2:]
    sign = sign_of(scal).astype(jnp.bfloat16)
    odd = scal[0] == 1
    start = 0
    for part in second_parts(scal, *refs[:-2]):
        rows = pl.ds(start, part.shape[0])
        one = first[rows, :]
        two = part * sign
        down_ref[0, rows, :] = jnp.where(odd, one, two)
        up_ref[0, rows, :] = jnp.where(odd, two, one)
        start += part.shape[0]


def on_device(down_state, up_state, reflectivity, w_down, w_up):
    level = lax.axis_index("depth")
    tile = lax.axis_index("lat")
    tiles = lax.axis_size("lat")
    columns, wide = down_state.shape[1:]
    scal = jnp.stack([level % 2, level, tile % 2]).astype(jnp.int32)
    inside = swap(*[(i, i + 1) for i in range(0, tiles, 2)])
    outside = swap(*[(i, i + 1) for i in range(1, tiles - 1, 2)])
    far = [pltpu.with_memory_space_constraint(x, pltpu.HBM) for x in (down_state, up_state, reflectivity, w_down, w_up)]
    sums = f32(2, 2 * columns, BLOCK)
    fields = pltpu.VMEM((2, columns, wide), jnp.bfloat16)
    for tick in range(TICKS):
        if tick == 0:
            e1, e2 = call(
                ends_start,
                (bf(2, columns, HALO),) * 2,
                (scal, *far[:3]),
                "ends",
                specs=[HBM] * 3,
                scratch=[
                    pltpu.VMEM((2, 2, columns, HALO), jnp.bfloat16),
                    pltpu.VMEM((1, wide), jnp.float32),
                    pltpu.SemaphoreType.DMA((5,)),
                ],
            )
        else:
            e1, e2 = call(ends_next, (bf(2, columns, HALO),) * 2, (scal, first, *second, reflectivity), "ends")
        if HFLIP and tick:
            h1 = lax.ppermute(e1, "lat", inside)
            h2 = lax.ppermute(e2, "lat", outside)
        else:
            h2 = lax.ppermute(e2, "lat", outside)
            h1 = lax.ppermute(e1, "lat", inside)
        if tick == 0:
            acc, weights = call(
                body_start,
                (sums, bf(2, 2 * BLOCK, BLOCK)),
                (scal, down_state, up_state, reflectivity, *far[3:]),
                "body",
                specs=[VMEM] * 3 + [HBM] * 2,
                scratch=[fields, pltpu.SemaphoreType.DMA((2,))],
            )
        else:
            (acc,) = call(body_next, (sums,), (scal, first, *second, reflectivity, weights), "body", scratch=[fields])
        *own, other = call(
            halo_dots,
            (bf(columns - STEP_ROWS, wide), bf(STEP_ROWS, wide), bf(columns, wide)),
            (scal, h1, h2, acc, weights),
            "edges",
        )
        first = lax.ppermute(other, "depth", SECOND)
        got_step = lax.ppermute(own[1], "depth", FIRST_STEP)
        got_direct = lax.ppermute(own[0], "depth", FIRST_DIRECT)
        got_forward = lax.ppermute(got_step, "depth", FIRST_FORWARD)
        second = (*own, got_direct, got_step, got_forward)
    return call(finish, (bf(1, columns, wide),) * 2, (scal, first, *second), "finish")


def solution(mesh):
    in_specs = (
        P("depth", None, "lat"),
        P("depth", None, "lat"),
        P("depth", "lat"),
        P("depth", "lat", None, None),
        P("depth", "lat", None, None),
    )
    out_specs = (P("depth", None, "lat"), P("depth", None, "lat"))
    return jax.shard_map(
        on_device, mesh=mesh, in_specs=in_specs, out_specs=out_specs, check_vma=False
    )
```

time: 238 us -> 188 us (0.79)
  the two profiles are of different devices: /device:TPU:199 before, /device:TPU:57 now
where the time goes in v2:
time: 188 us; the launch traced here: 187 us
  waiting for transfers between devices  94.4 us (50%)
  starting transfers between devices  62.7 us (33%)
  Pallas kernels  29.2 us (16%)
    ppermute x4, waiting for transfers between devices, on_device(): got_forward = lax.ppermute(got_step, 'depth', FIRST_FORWARD)  44.8 us
    ppermute x4, waiting for transfers between devices, on_device(): got_direct = lax.ppermute(own[0], 'depth', FIRST_DIRECT)  37 us
    ppermute x4, starting transfers between devices, on_device(): got_direct = lax.ppermute(own[0], 'depth', FIRST_DIRECT)  33.8 us
    pallas_call x13, Pallas kernels, call(): pl.pallas_call(body, out_shape=tuple(outs), in_specs=[SMEM] + (specs or [...  29.2 us
    ppermute x4, waiting for transfers between devices, on_device(): h2 = lax.ppermute(e2, 'lat', outside)  12.5 us
    ppermute x4, starting transfers between devices, on_device(): h2 = lax.ppermute(e2, 'lat', outside)  9.51 us
    ppermute x4, starting transfers between devices, on_device(): h1 = lax.ppermute(e1, 'lat', inside)  6.84 us
    ppermute x4, starting transfers between devices, on_device(): got_step = lax.ppermute(own[1], 'depth', FIRST_STEP)  6.6 us
  transfers between devices with their start and end apart: 24, of which 11 were waited for; matrix products, arithmetic and copies ran while one was open for 0% of the time, Pallas kernels for 8%

profile of v2, /device:TPU:57, one launch (start us, length us, event | category | flops | bytes accessed | tf_op | source)
XLA Modules:
  0.0 187.3 jit_solution(3468773357046332948)
XLA Ops:
  0.7 2.4 %ends.4 = (bf16[2,192,512]{2,1,0:T(8,128)(2,1)S(1)}, bf16[2,192,512]{2,1,0:T(8,128)(2,1)S(1)}) custom-call(s32[3]{0:T(128)S(1)} %pad_add_fusion.scal, bf16[1,192,2048]{2,1,0:T(8,128)(2,1)} %down.3, bf16[1,192,2048]{2,1,0:T(8,128)(2,1)} %up.3, f32[1,2048]{1,0:T(1,128)} %refs_5_.11), custom_call_target="tpu_custom_call" | custom-call | flops 10000000000 | bytes 1 | tf_op jit(solution)/shard_map/ends/pallas_call | solution.py:43
  3.9 3.0 %collective-permute-start.1 = (bf16[2,192,512]{2,1,0:T(8,128)(2,1)S(1)}, bf16[2,192,512]{2,1,0:T(8,128)(2,1)S(1)}, u32[]{:S(2)}, u32[]{:S(2)}) collective-permute-start(bf16[2,192,512]{2,1,0:T(8,128)(2,1)S(1)} %get-tuple-element.25), channel_id=1, source_target_pairs={{1,2},{2,1},{3,4},{4,3},{5,6},{6,5},{7,8},{8,7},{9,10},{10,9},{11,... | collective-permute-start | bytes 1179656 | tf_op jit(solution)/shard_map/ppermute | solution.py:250
  6.9 5.6 %body.4 = (f32[2,384,1024]{2,1,0:T(8,128)S(1)}, bf16[2,2048,1024]{2,1,0:T(8,128)(2,1)S(1)}) custom-call(s32[3]{0:T(128)S(1)} %pad_add_fusion.scal, bf16[1,192,2048]{2,1,0:T(8,128)(2,1)S(1)} %copy-done, bf16[1,192,2048]{2,1,0:T(8,128)(2,1)S(1)} %copy-done.1, f32[1,2048]{1,0:T(1,128)S(1)} %copy-done.2, bf16[1,1,2048,1024]{3,2,1,0:T(8,128)(2,1)} %w_down.1, ...), custom_call_target="tpu_custom_call" | custom-call | flops 10000000000 | bytes 1 | tf_op jit(solution)/shard_map/body/pallas_call | solution.py:43
  13.2 1.6 edges.4
  15.4 2.7 %collective-permute-start.4 = (bf16[64,2048]{1,0:T(8,128)(2,1)S(1)}, bf16[64,2048]{1,0:T(8,128)(2,1)S(1)}, u32[]{:S(2)}, u32[]{:S(2)}) collective-permute-start(bf16[64,2048]{1,0:T(8,128)(2,1)S(1)} %get-tuple-element.30.refs_1_), channel_id=1, source_target_pairs={{32,64},{64,32},{160,192},{192,160},{96,0},{128,224},{33,65},{65,3... | collective-permute-start | bytes 786440 | tf_op jit(solution)/shard_map/ppermute | solution.py:270
  18.1 9.5 %collective-permute-start.3 = (bf16[128,2048]{1,0:T(8,128)(2,1)S(1)}, bf16[128,2048]{1,0:T(8,128)(2,1)S(1)}, u32[]{:S(2)}, u32[]{:S(2)}) collective-permute-start(bf16[128,2048]{1,0:T(8,128)(2,1)S(1)} %get-tuple-element.29.refs_0_), channel_id=1, source_target_pairs={{32,64},{64,32},{160,192},{192,160},{96,128},{128,96},{33,65},{65,... | collective-permute-start | bytes 1572872 | tf_op jit(solution)/shard_map/ppermute | solution.py:271
  29.0 17.4 %collective-permute-done.5.refs_4_ = bf16[64,2048]{1,0:T(8,128)(2,1)S(1)} collective-permute-done((bf16[64,2048]{1,0:T(8,128)(2,1)S(1)}, bf16[64,2048]{1,0:T(8,128)(2,1)S(1)}, u32[]{:S(2)}, u32[]{:S(2)}) %collective-permute-start.5) | collective-permute-done | bytes 262176 | tf_op jit(solution)/shard_map/ppermute | solution.py:272
  46.4 3.2 %collective-permute-done.3.refs_2_ = bf16[128,2048]{1,0:T(8,128)(2,1)S(1)} collective-permute-done((bf16[128,2048]{1,0:T(8,128)(2,1)S(1)}, bf16[128,2048]{1,0:T(8,128)(2,1)S(1)}, u32[]{:S(2)}, u32[]{:S(2)}) %collective-permute-start.3) | collective-permute-done | bytes 524320 | tf_op jit(solution)/shard_map/ppermute | solution.py:271
  50.6 2.4 %collective-permute-start.6 = (bf16[2,192,512]{2,1,0:T(8,128)(2,1)S(1)}, bf16[2,192,512]{2,1,0:T(8,128)(2,1)S(1)}, u32[]{:S(2)}, u32[]{:S(2)}) collective-permute-start(bf16[2,192,512]{2,1,0:T(8,128)(2,1)S(1)} %get-tuple-element.31), channel_id=1, source_target_pairs={{0,1},{1,0},{2,3},{3,2},{4,5},{5,4},{6,7},{7,6},{8,9},{9,8},{10,11... | collective-permute-start | bytes 1179656 | tf_op jit(solution)/shard_map/ppermute | solution.py:251
  52.9 2.7 %collective-permute-start.7 = (bf16[2,192,512]{2,1,0:T(8,128)(2,1)S(1)}, bf16[2,192,512]{2,1,0:T(8,128)(2,1)S(1)}, u32[]{:S(2)}, u32[]{:S(2)}) collective-permute-start(bf16[2,192,512]{2,1,0:T(8,128)(2,1)S(1)} %get-tuple-element.32), channel_id=1, source_target_pairs={{1,2},{2,1},{3,4},{4,3},{5,6},{6,5},{7,8},{8,7},{9,10},{10,9},{11,... | collective-permute-start | bytes 1179656 | tf_op jit(solution)/shard_map/ppermute | solution.py:250
  55.6 3.3 %body.5.acc_ref = f32[2,384,1024]{2,1,0:T(8,128)S(1)} custom-call(s32[3]{0:T(128)S(1)} %pad_add_fusion.scal, bf16[192,2048]{1,0:T(8,128)(2,1)S(1)} %collective-permute-done.2.first, bf16[128,2048]{1,0:T(8,128)(2,1)S(1)} %get-tuple-element.29.refs_0_, bf16[64,2048]{1,0:T(8,128)(2,1)S(1)} %get-tuple-element.30.refs_1_, ...), custom_call_target="tpu_custom_call" | custom-call | flops 10000000000 | bytes 1 | tf_op jit(solution)/shard_map/body/pallas_call | solution.py:43
  58.9 3.4 %collective-permute-done.7.h2_ref = bf16[2,192,512]{2,1,0:T(8,128)(2,1)S(1)} collective-permute-done((bf16[2,192,512]{2,1,0:T(8,128)(2,1)S(1)}, bf16[2,192,512]{2,1,0:T(8,128)(2,1)S(1)}, u32[]{:S(2)}, u32[]{:S(2)}) %collective-permute-start.7) | collective-permute-done | bytes 393248 | tf_op jit(solution)/shard_map/ppermute | solution.py:250
  62.3 1.6 edges.5
  65.4 9.4 %collective-permute-start.9 = (bf16[128,2048]{1,0:T(8,128)(2,1)S(1)}, bf16[128,2048]{1,0:T(8,128)(2,1)S(1)}, u32[]{:S(2)}, u32[]{:S(2)}) collective-permute-start(bf16[128,2048]{1,0:T(8,128)(2,1)S(1)} %get-tuple-element.34.refs_0_), channel_id=1, source_target_pairs={{32,64},{64,32},{160,192},{192,160},{96,128},{128,96},{33,65},{65,... | collective-permute-start | bytes 1572872 | tf_op jit(solution)/shard_map/ppermute | solution.py:271
  76.1 10.2 %collective-permute-done.11.refs_4_ = bf16[64,2048]{1,0:T(8,128)(2,1)S(1)} collective-permute-done((bf16[64,2048]{1,0:T(8,128)(2,1)S(1)}, bf16[64,2048]{1,0:T(8,128)(2,1)S(1)}, u32[]{:S(2)}, u32[]{:S(2)}) %collective-permute-start.11) | collective-permute-done | bytes 262176 | tf_op jit(solution)/shard_map/ppermute | solution.py:272
  86.3 8.1 %collective-permute-done.9.refs_2_ = bf16[128,2048]{1,0:T(8,128)(2,1)S(1)} collective-permute-done((bf16[128,2048]{1,0:T(8,128)(2,1)S(1)}, bf16[128,2048]{1,0:T(8,128)(2,1)S(1)}, u32[]{:S(2)}, u32[]{:S(2)}) %collective-permute-start.9) | collective-permute-done | bytes 524320 | tf_op jit(solution)/shard_map/ppermute | solution.py:271
  96.6 1.9 %collective-permute-start.13 = (bf16[2,192,512]{2,1,0:T(8,128)(2,1)S(1)}, bf16[2,192,512]{2,1,0:T(8,128)(2,1)S(1)}, u32[]{:S(2)}, u32[]{:S(2)}) collective-permute-start(bf16[2,192,512]{2,1,0:T(8,128)(2,1)S(1)} %get-tuple-element.37), channel_id=1, source_target_pairs={{1,2},{2,1},{3,4},{4,3},{5,6},{6,5},{7,8},{8,7},{9,10},{10,9},{11,... | collective-permute-start | bytes 1179656 | tf_op jit(solution)/shard_map/ppermute | solution.py:250
  98.5 3.3 %body.6.acc_ref = f32[2,384,1024]{2,1,0:T(8,128)S(1)} custom-call(s32[3]{0:T(128)S(1)} %pad_add_fusion.scal, bf16[192,2048]{1,0:T(8,128)(2,1)S(1)} %collective-permute-done.8.first, bf16[128,2048]{1,0:T(8,128)(2,1)S(1)} %get-tuple-element.34.refs_0_, bf16[64,2048]{1,0:T(8,128)(2,1)S(1)} %get-tuple-element.35.refs_1_, ...), custom_call_target="tpu_custom_call" | custom-call | flops 10000000000 | bytes 1 | tf_op jit(solution)/shard_map/body/pallas_call | solution.py:43
  101.8 4.2 %collective-permute-done.13.h2_ref = bf16[2,192,512]{2,1,0:T(8,128)(2,1)S(1)} collective-permute-done((bf16[2,192,512]{2,1,0:T(8,128)(2,1)S(1)}, bf16[2,192,512]{2,1,0:T(8,128)(2,1)S(1)}, u32[]{:S(2)}, u32[]{:S(2)}) %collective-permute-start.13) | collective-permute-done | bytes 393248 | tf_op jit(solution)/shard_map/ppermute | solution.py:250
  106.0 1.6 edges.6
  109.0 7.4 %collective-permute-start.15 = (bf16[128,2048]{1,0:T(8,128)(2,1)S(1)}, bf16[128,2048]{1,0:T(8,128)(2,1)S(1)}, u32[]{:S(2)}, u32[]{:S(2)}) collective-permute-start(bf16[128,2048]{1,0:T(8,128)(2,1)S(1)} %get-tuple-element.39.refs_0_), channel_id=1, source_target_pairs={{32,64},{64,32},{160,192},{192,160},{96,128},{128,96},{33,65},{65,... | collective-permute-start | bytes 1572872 | tf_op jit(solution)/shard_map/ppermute | solution.py:271
  117.7 17.2 %collective-permute-done.17.refs_4_ = bf16[64,2048]{1,0:T(8,128)(2,1)S(1)} collective-permute-done((bf16[64,2048]{1,0:T(8,128)(2,1)S(1)}, bf16[64,2048]{1,0:T(8,128)(2,1)S(1)}, u32[]{:S(2)}, u32[]{:S(2)}) %collective-permute-start.17) | collective-permute-done | bytes 262176 | tf_op jit(solution)/shard_map/ppermute | solution.py:272
  135.0 5.2 %collective-permute-done.15.refs_2_ = bf16[128,2048]{1,0:T(8,128)(2,1)S(1)} collective-permute-done((bf16[128,2048]{1,0:T(8,128)(2,1)S(1)}, bf16[128,2048]{1,0:T(8,128)(2,1)S(1)}, u32[]{:S(2)}, u32[]{:S(2)}) %collective-permute-start.15) | collective-permute-done | bytes 524320 | tf_op jit(solution)/shard_map/ppermute | solution.py:271
  141.3 2.5 %collective-permute-start.18 = (bf16[2,192,512]{2,1,0:T(8,128)(2,1)S(1)}, bf16[2,192,512]{2,1,0:T(8,128)(2,1)S(1)}, u32[]{:S(2)}, u32[]{:S(2)}) collective-permute-start(bf16[2,192,512]{2,1,0:T(8,128)(2,1)S(1)} %get-tuple-element.41), channel_id=1, source_target_pairs={{0,1},{1,0},{2,3},{3,2},{4,5},{5,4},{6,7},{7,6},{8,9},{9,8},{10,11... | collective-permute-start | bytes 1179656 | tf_op jit(solution)/shard_map/ppermute | solution.py:251
  143.7 1.9 %collective-permute-start.19 = (bf16[2,192,512]{2,1,0:T(8,128)(2,1)S(1)}, bf16[2,192,512]{2,1,0:T(8,128)(2,1)S(1)}, u32[]{:S(2)}, u32[]{:S(2)}) collective-permute-start(bf16[2,192,512]{2,1,0:T(8,128)(2,1)S(1)} %get-tuple-element.42), channel_id=1, source_target_pairs={{1,2},{2,1},{3,4},{4,3},{5,6},{6,5},{7,8},{8,7},{9,10},{10,9},{11,... | collective-permute-start | bytes 1179656 | tf_op jit(solution)/shard_map/ppermute | solution.py:250
  145.7 3.2 %body.7.acc_ref = f32[2,384,1024]{2,1,0:T(8,128)S(1)} custom-call(s32[3]{0:T(128)S(1)} %pad_add_fusion.scal, bf16[192,2048]{1,0:T(8,128)(2,1)S(1)} %collective-permute-done.14.first, bf16[128,2048]{1,0:T(8,128)(2,1)S(1)} %get-tuple-element.39.refs_0_, bf16[64,2048]{1,0:T(8,128)(2,1)S(1)} %get-tuple-element.40.refs_1_, ...), custom_call_target="tpu_custom_call" | custom-call | flops 10000000000 | bytes 1 | tf_op jit(solution)/shard_map/body/pallas_call | solution.py:43
  148.9 4.2 %collective-permute-done.19.h2_ref = bf16[2,192,512]{2,1,0:T(8,128)(2,1)S(1)} collective-permute-done((bf16[2,192,512]{2,1,0:T(8,128)(2,1)S(1)}, bf16[2,192,512]{2,1,0:T(8,128)(2,1)S(1)}, u32[]{:S(2)}, u32[]{:S(2)}) %collective-permute-start.19) | collective-permute-done | bytes 393248 | tf_op jit(solution)/shard_map/ppermute | solution.py:250
  153.1 1.6 edges.7
  154.9 1.3 collective-permute-start.22
  156.2 7.4 %collective-permute-start.21 = (bf16[128,2048]{1,0:T(8,128)(2,1)S(1)}, bf16[128,2048]{1,0:T(8,128)(2,1)S(1)}, u32[]{:S(2)}, u32[]{:S(2)}) collective-permute-start(bf16[128,2048]{1,0:T(8,128)(2,1)S(1)} %get-tuple-element.44.refs_0_), channel_id=1, source_target_pairs={{32,64},{64,32},{160,192},{192,160},{96,128},{128,96},{33,65},{65,... | collective-permute-start | bytes 1572872 | tf_op jit(solution)/shard_map/ppermute | solution.py:271
  164.9 20.5 %collective-permute-done.21.refs_2_ = bf16[128,2048]{1,0:T(8,128)(2,1)S(1)} collective-permute-done((bf16[128,2048]{1,0:T(8,128)(2,1)S(1)}, bf16[128,2048]{1,0:T(8,128)(2,1)S(1)}, u32[]{:S(2)}, u32[]{:S(2)}) %collective-permute-start.21) | collective-permute-done | bytes 524320 | tf_op jit(solution)/shard_map/ppermute | solution.py:271
  185.4 1.9 %finish.1 = (bf16[1,192,2048]{2,1,0:T(8,128)(2,1)}, bf16[1,192,2048]{2,1,0:T(8,128)(2,1)}) custom-call(s32[3]{0:T(128)S(1)} %pad_add_fusion.scal, bf16[192,2048]{1,0:T(8,128)(2,1)S(1)} %collective-permute-done.20.first, bf16[128,2048]{1,0:T(8,128)(2,1)S(1)} %get-tuple-element.44.refs_0_, bf16[64,2048]{1,0:T(8,128)(2,1)S(1)} %get-tuple-element.45.refs_1_, ...), custom_call_target="tpu_custom_call" | custom-call | flops 10000000000 | bytes 1 | tf_op jit(solution)/shard_map/finish/pallas_call | solution.py:43
  (36 shorter events, 14.5 us)
Async XLA Ops:
  0.7 6.2 %copy-start = (bf16[1,192,2048]{2,1,0:T(8,128)(2,1)S(1)}, bf16[1,192,2048]{2,1,0:T(8,128)(2,1)}, u32[]{:S(2)}) copy-start(bf16[1,192,2048]{2,1,0:T(8,128)(2,1)} %down.3) | copy-start | bytes 2359300
  0.7 6.2 %copy-start.1 = (bf16[1,192,2048]{2,1,0:T(8,128)(2,1)S(1)}, bf16[1,192,2048]{2,1,0:T(8,128)(2,1)}, u32[]{:S(2)}) copy-start(bf16[1,192,2048]{2,1,0:T(8,128)(2,1)} %up.3) | copy-start | bytes 2359300
  0.7 6.2 %copy-start.2 = (f32[1,2048]{1,0:T(1,128)S(1)}, f32[1,2048]{1,0:T(1,128)}, u32[]{:S(2)}) copy-start(f32[1,2048]{1,0:T(1,128)} %refs_5_.11) | copy-start | bytes 24580
  3.1 9.4 %collective-permute-start = (bf16[2,192,512]{2,1,0:T(8,128)(2,1)S(1)}, bf16[2,192,512]{2,1,0:T(8,128)(2,1)S(1)}, u32[]{:S(2)}, u32[]{:S(2)}) collective-permute-start(bf16[2,192,512]{2,1,0:T(8,128)(2,1)S(1)} %get-tuple-element.24), channel_id=1, source_target_pairs={{0,1},{1,0},{2,3},{3,2},{4,5},{5,4},{6,7},{7,6},{8,9},{9,8},{10,11... | collective-permute-start | bytes 1179656 | tf_op jit(solution)/shard_map/ppermute | solution.py:251
  3.9 9.4 %collective-permute-start.1 = (bf16[2,192,512]{2,1,0:T(8,128)(2,1)S(1)}, bf16[2,192,512]{2,1,0:T(8,128)(2,1)S(1)}, u32[]{:S(2)}, u32[]{:S(2)}) collective-permute-start(bf16[2,192,512]{2,1,0:T(8,128)(2,1)S(1)} %get-tuple-element.25), channel_id=1, source_target_pairs={{1,2},{2,1},{3,4},{4,3},{5,6},{6,5},{7,8},{8,7},{9,10},{10,9},{11,... | collective-permute-start | bytes 1179656 | tf_op jit(solution)/shard_map/ppermute | solution.py:250
  14.9 34.7 %collective-permute-start.2 = (bf16[192,2048]{1,0:T(8,128)(2,1)S(1)}, bf16[192,2048]{1,0:T(8,128)(2,1)S(1)}, u32[]{:S(2)}, u32[]{:S(2)}) collective-permute-start(bf16[192,2048]{1,0:T(8,128)(2,1)S(1)} %get-tuple-element.28), channel_id=1, source_target_pairs={{0,32},{32,0},{64,96},{96,64},{128,160},{160,128},{192,224},{224,1... | collective-permute-start | bytes 2359304 | tf_op jit(solution)/shard_map/ppermute | solution.py:269
  15.4 12.2 %collective-permute-start.4 = (bf16[64,2048]{1,0:T(8,128)(2,1)S(1)}, bf16[64,2048]{1,0:T(8,128)(2,1)S(1)}, u32[]{:S(2)}, u32[]{:S(2)}) collective-permute-start(bf16[64,2048]{1,0:T(8,128)(2,1)S(1)} %get-tuple-element.30.refs_1_), channel_id=1, source_target_pairs={{32,64},{64,32},{160,192},{192,160},{96,0},{128,224},{33,65},{65,3... | collective-permute-start | bytes 786440 | tf_op jit(solution)/shard_map/ppermute | solution.py:270
  18.1 31.4 %collective-permute-start.3 = (bf16[128,2048]{1,0:T(8,128)(2,1)S(1)}, bf16[128,2048]{1,0:T(8,128)(2,1)S(1)}, u32[]{:S(2)}, u32[]{:S(2)}) collective-permute-start(bf16[128,2048]{1,0:T(8,128)(2,1)S(1)} %get-tuple-element.29.refs_0_), channel_id=1, source_target_pairs={{32,64},{64,32},{160,192},{192,160},{96,128},{128,96},{33,65},{65,... | collective-permute-start | bytes 1572872 | tf_op jit(solution)/shard_map/ppermute | solution.py:271
  27.7 18.7 %collective-permute-start.5 = (bf16[64,2048]{1,0:T(8,128)(2,1)S(1)}, bf16[64,2048]{1,0:T(8,128)(2,1)S(1)}, u32[]{:S(2)}, u32[]{:S(2)}) collective-permute-start(bf16[64,2048]{1,0:T(8,128)(2,1)S(1)} %collective-permute-done.4.refs_3_), channel_id=1, source_target_pairs={{0,128},{224,96},{1,129},{225,97},{2,130},{226,98},{3,131},{227,99... | collective-permute-start | bytes 786440 | tf_op jit(solution)/shard_map/ppermute | solution.py:272
  50.6 8.3 %collective-permute-start.6 = (bf16[2,192,512]{2,1,0:T(8,128)(2,1)S(1)}, bf16[2,192,512]{2,1,0:T(8,128)(2,1)S(1)}, u32[]{:S(2)}, u32[]{:S(2)}) collective-permute-start(bf16[2,192,512]{2,1,0:T(8,128)(2,1)S(1)} %get-tuple-element.31), channel_id=1, source_target_pairs={{0,1},{1,0},{2,3},{3,2},{4,5},{5,4},{6,7},{7,6},{8,9},{9,8},{10,11... | collective-permute-start | bytes 1179656 | tf_op jit(solution)/shard_map/ppermute | solution.py:251
  52.9 9.4 %collective-permute-start.7 = (bf16[2,192,512]{2,1,0:T(8,128)(2,1)S(1)}, bf16[2,192,512]{2,1,0:T(8,128)(2,1)S(1)}, u32[]{:S(2)}, u32[]{:S(2)}) collective-permute-start(bf16[2,192,512]{2,1,0:T(8,128)(2,1)S(1)} %get-tuple-element.32), channel_id=1, source_target_pairs={{1,2},{2,1},{3,4},{4,3},{5,6},{6,5},{7,8},{8,7},{9,10},{10,9},{11,... | collective-permute-start | bytes 1179656 | tf_op jit(solution)/shard_map/ppermute | solution.py:250
  63.9 30.4 %collective-permute-start.8 = (bf16[192,2048]{1,0:T(8,128)(2,1)S(1)}, bf16[192,2048]{1,0:T(8,128)(2,1)S(1)}, u32[]{:S(2)}, u32[]{:S(2)}) collective-permute-start(bf16[192,2048]{1,0:T(8,128)(2,1)S(1)} %get-tuple-element.33), channel_id=1, source_target_pairs={{0,32},{32,0},{64,96},{96,64},{128,160},{160,128},{192,224},{224,1... | collective-permute-start | bytes 2359304 | tf_op jit(solution)/shard_map/ppermute | solution.py:269
  64.0 10.8 %collective-permute-start.10 = (bf16[64,2048]{1,0:T(8,128)(2,1)S(1)}, bf16[64,2048]{1,0:T(8,128)(2,1)S(1)}, u32[]{:S(2)}, u32[]{:S(2)}) collective-permute-start(bf16[64,2048]{1,0:T(8,128)(2,1)S(1)} %get-tuple-element.35.refs_1_), channel_id=1, source_target_pairs={{32,64},{64,32},{160,192},{192,160},{96,0},{128,224},{33,65},{65,3... | collective-permute-start | bytes 786440 | tf_op jit(solution)/shard_map/ppermute | solution.py:270
  65.4 29.0 %collective-permute-start.9 = (bf16[128,2048]{1,0:T(8,128)(2,1)S(1)}, bf16[128,2048]{1,0:T(8,128)(2,1)S(1)}, u32[]{:S(2)}, u32[]{:S(2)}) collective-permute-start(bf16[128,2048]{1,0:T(8,128)(2,1)S(1)} %get-tuple-element.34.refs_0_), channel_id=1, source_target_pairs={{32,64},{64,32},{160,192},{192,160},{96,128},{128,96},{33,65},{65,... | collective-permute-start | bytes 1572872 | tf_op jit(solution)/shard_map/ppermute | solution.py:271
  74.8 11.5 %collective-permute-start.11 = (bf16[64,2048]{1,0:T(8,128)(2,1)S(1)}, bf16[64,2048]{1,0:T(8,128)(2,1)S(1)}, u32[]{:S(2)}, u32[]{:S(2)}) collective-permute-start(bf16[64,2048]{1,0:T(8,128)(2,1)S(1)} %collective-permute-done.10.refs_3_), channel_id=1, source_target_pairs={{0,128},{224,96},{1,129},{225,97},{2,130},{226,98},{3,131},{227,99... | collective-permute-start | bytes 786440 | tf_op jit(solution)/shard_map/ppermute | solution.py:272
  95.4 6.4 %collective-permute-start.12 = (bf16[2,192,512]{2,1,0:T(8,128)(2,1)S(1)}, bf16[2,192,512]{2,1,0:T(8,128)(2,1)S(1)}, u32[]{:S(2)}, u32[]{:S(2)}) collective-permute-start(bf16[2,192,512]{2,1,0:T(8,128)(2,1)S(1)} %get-tuple-element.36), channel_id=1, source_target_pairs={{0,1},{1,0},{2,3},{3,2},{4,5},{5,4},{6,7},{7,6},{8,9},{9,8},{10,11... | collective-permute-start | bytes 1179656 | tf_op jit(solution)/shard_map/ppermute | solution.py:251
  96.6 9.4 %collective-permute-start.13 = (bf16[2,192,512]{2,1,0:T(8,128)(2,1)S(1)}, bf16[2,192,512]{2,1,0:T(8,128)(2,1)S(1)}, u32[]{:S(2)}, u32[]{:S(2)}) collective-permute-start(bf16[2,192,512]{2,1,0:T(8,128)(2,1)S(1)} %get-tuple-element.37), channel_id=1, source_target_pairs={{1,2},{2,1},{3,4},{4,3},{5,6},{6,5},{7,8},{8,7},{9,10},{10,9},{11,... | collective-permute-start | bytes 1179656 | tf_op jit(solution)/shard_map/ppermute | solution.py:250
  107.6 32.6 %collective-permute-start.14 = (bf16[192,2048]{1,0:T(8,128)(2,1)S(1)}, bf16[192,2048]{1,0:T(8,128)(2,1)S(1)}, u32[]{:S(2)}, u32[]{:S(2)}) collective-permute-start(bf16[192,2048]{1,0:T(8,128)(2,1)S(1)} %get-tuple-element.38), channel_id=1, source_target_pairs={{0,32},{32,0},{64,96},{96,64},{128,160},{160,128},{192,224},{224,1... | collective-permute-start | bytes 2359304 | tf_op jit(solution)/shard_map/ppermute | solution.py:269
  107.7 8.7 %collective-permute-start.16 = (bf16[64,2048]{1,0:T(8,128)(2,1)S(1)}, bf16[64,2048]{1,0:T(8,128)(2,1)S(1)}, u32[]{:S(2)}, u32[]{:S(2)}) collective-permute-start(bf16[64,2048]{1,0:T(8,128)(2,1)S(1)} %get-tuple-element.40.refs_1_), channel_id=1, source_target_pairs={{32,64},{64,32},{160,192},{192,160},{96,0},{128,224},{33,65},{65,3... | collective-permute-start | bytes 786440 | tf_op jit(solution)/shard_map/ppermute | solution.py:270
  109.0 31.2 %collective-permute-start.15 = (bf16[128,2048]{1,0:T(8,128)(2,1)S(1)}, bf16[128,2048]{1,0:T(8,128)(2,1)S(1)}, u32[]{:S(2)}, u32[]{:S(2)}) collective-permute-start(bf16[128,2048]{1,0:T(8,128)(2,1)S(1)} %get-tuple-element.39.refs_0_), channel_id=1, source_target_pairs={{32,64},{64,32},{160,192},{192,160},{96,128},{128,96},{33,65},{65,... | collective-permute-start | bytes 1572872 | tf_op jit(solution)/shard_map/ppermute | solution.py:271
  116.4 18.5 %collective-permute-start.17 = (bf16[64,2048]{1,0:T(8,128)(2,1)S(1)}, bf16[64,2048]{1,0:T(8,128)(2,1)S(1)}, u32[]{:S(2)}, u32[]{:S(2)}) collective-permute-start(bf16[64,2048]{1,0:T(8,128)(2,1)S(1)} %collective-permute-done.16.refs_3_), channel_id=1, source_target_pairs={{0,128},{224,96},{1,129},{225,97},{2,130},{226,98},{3,131},{227,99... | collective-permute-start | bytes 786440 | tf_op jit(solution)/shard_map/ppermute | solution.py:272
  141.3 7.7 %collective-permute-start.18 = (bf16[2,192,512]{2,1,0:T(8,128)(2,1)S(1)}, bf16[2,192,512]{2,1,0:T(8,128)(2,1)S(1)}, u32[]{:S(2)}, u32[]{:S(2)}) collective-permute-start(bf16[2,192,512]{2,1,0:T(8,128)(2,1)S(1)} %get-tuple-element.41), channel_id=1, source_target_pairs={{0,1},{1,0},{2,3},{3,2},{4,5},{5,4},{6,7},{7,6},{8,9},{9,8},{10,11... | collective-permute-start | bytes 1179656 | tf_op jit(solution)/shard_map/ppermute | solution.py:251
  143.7 9.4 %collective-permute-start.19 = (bf16[2,192,512]{2,1,0:T(8,128)(2,1)S(1)}, bf16[2,192,512]{2,1,0:T(8,128)(2,1)S(1)}, u32[]{:S(2)}, u32[]{:S(2)}) collective-permute-start(bf16[2,192,512]{2,1,0:T(8,128)(2,1)S(1)} %get-tuple-element.42), channel_id=1, source_target_pairs={{1,2},{2,1},{3,4},{4,3},{5,6},{6,5},{7,8},{8,7},{9,10},{10,9},{11,... | collective-permute-start | bytes 1179656 | tf_op jit(solution)/shard_map/ppermute | solution.py:250
  154.8 30.7 %collective-permute-start.20 = (bf16[192,2048]{1,0:T(8,128)(2,1)S(1)}, bf16[192,2048]{1,0:T(8,128)(2,1)S(1)}, u32[]{:S(2)}, u32[]{:S(2)}) collective-permute-start(bf16[192,2048]{1,0:T(8,128)(2,1)S(1)} %get-tuple-element.43), channel_id=1, source_target_pairs={{0,32},{32,0},{64,96},{96,64},{128,160},{160,128},{192,224},{224,1... | collective-permute-start | bytes 2359304 | tf_op jit(solution)/shard_map/ppermute | solution.py:269
  154.9 8.8 %collective-permute-start.22 = (bf16[64,2048]{1,0:T(8,128)(2,1)S(1)}, bf16[64,2048]{1,0:T(8,128)(2,1)S(1)}, u32[]{:S(2)}, u32[]{:S(2)}) collective-permute-start(bf16[64,2048]{1,0:T(8,128)(2,1)S(1)} %get-tuple-element.45.refs_1_), channel_id=1, source_target_pairs={{32,64},{64,32},{160,192},{192,160},{96,0},{128,224},{33,65},{65,3... | collective-permute-start | bytes 786440 | tf_op jit(solution)/shard_map/ppermute | solution.py:270
  156.2 29.2 %collective-permute-start.21 = (bf16[128,2048]{1,0:T(8,128)(2,1)S(1)}, bf16[128,2048]{1,0:T(8,128)(2,1)S(1)}, u32[]{:S(2)}, u32[]{:S(2)}) collective-permute-start(bf16[128,2048]{1,0:T(8,128)(2,1)S(1)} %get-tuple-element.44.refs_0_), channel_id=1, source_target_pairs={{32,64},{64,32},{160,192},{192,160},{96,128},{128,96},{33,65},{65,... | collective-permute-start | bytes 1572872 | tf_op jit(solution)/shard_map/ppermute | solution.py:271
  163.6 21.8 %collective-permute-start.23 = (bf16[64,2048]{1,0:T(8,128)(2,1)S(1)}, bf16[64,2048]{1,0:T(8,128)(2,1)S(1)}, u32[]{:S(2)}, u32[]{:S(2)}) collective-permute-start(bf16[64,2048]{1,0:T(8,128)(2,1)S(1)} %collective-permute-done.22.refs_3_), channel_id=1, source_target_pairs={{0,128},{224,96},{1,129},{225,97},{2,130},{226,98},{3,131},{227,99... | collective-permute-start | bytes 786440 | tf_op jit(solution)/shard_map/ppermute | solution.py:272

commit v3 on v2

--- a/solution.py
+++ b/solution.py
@@ -9,14 +9,11 @@
 
 BLOCK = 1024
 HALO = 512
-TICKS = 4
-STEP_ROWS = 64
-HFLIP = False
+STEP_ROWS = (80, 64, 64, 80)
 GRANT = 20 * 1024 * 1024
 HINT = 10_000_000_000
 
 VMEM = pl.BlockSpec(memory_space=pltpu.VMEM)
-SMEM = pl.BlockSpec(memory_space=pltpu.SMEM)
 HBM = pl.BlockSpec(memory_space=pltpu.HBM)
 
 
@@ -40,10 +37,14 @@
 
 
 def call(body, outs, ins, name, specs=None, scratch=(), out_specs=None, aliases=None):
+    def kernel(*refs):
+        level = lax.axis_index("depth")
+        body((level % 2, level, lax.axis_index("lat") % 2), *refs)
+
     return pl.pallas_call(
-        body,
+        kernel,
         out_shape=tuple(outs),
-        in_specs=[SMEM] + (specs or [VMEM] * (len(ins) - 1)),
+        in_specs=specs or [VMEM] * len(ins),
         out_specs=out_specs or tuple(VMEM for _ in outs),
         scratch_shapes=scratch,
         input_output_aliases=aliases or {},
@@ -217,22 +218,19 @@
 
 
 def on_device(down_state, up_state, reflectivity, w_down, w_up):
-    level = lax.axis_index("depth")
-    tile = lax.axis_index("lat")
     tiles = lax.axis_size("lat")
     columns, wide = down_state.shape[1:]
-    scal = jnp.stack([level % 2, level, tile % 2]).astype(jnp.int32)
     inside = swap(*[(i, i + 1) for i in range(0, tiles, 2)])
     outside = swap(*[(i, i + 1) for i in range(1, tiles - 1, 2)])
     far = [pltpu.with_memory_space_constraint(x, pltpu.HBM) for x in (down_state, up_state, reflectivity, w_down, w_up)]
     sums = f32(2, 2 * columns, BLOCK)
     fields = pltpu.VMEM((2, columns, wide), jnp.bfloat16)
-    for tick in range(TICKS):
+    for tick in range(len(STEP_ROWS)):
         if tick == 0:
             e1, e2 = call(
                 ends_start,
                 (bf(2, columns, HALO),) * 2,
-                (scal, *far[:3]),
+                tuple(far[:3]),
                 "ends",
                 specs=[HBM] * 3,
                 scratch=[
@@ -242,28 +240,24 @@
                 ],
             )
         else:
-            e1, e2 = call(ends_next, (bf(2, columns, HALO),) * 2, (scal, first, *second, reflectivity), "ends")
-        if HFLIP and tick:
-            h1 = lax.ppermute(e1, "lat", inside)
-            h2 = lax.ppermute(e2, "lat", outside)
-        else:
-            h2 = lax.ppermute(e2, "lat", outside)
-            h1 = lax.ppermute(e1, "lat", inside)
+            e1, e2 = call(ends_next, (bf(2, columns, HALO),) * 2, (first, *second, reflectivity), "ends")
+        h2 = lax.ppermute(e2, "lat", outside)
+        h1 = lax.ppermute(e1, "lat", inside)
         if tick == 0:
             acc, weights = call(
                 body_start,
                 (sums, bf(2, 2 * BLOCK, BLOCK)),
-                (scal, down_state, up_state, reflectivity, *far[3:]),
+                (down_state, up_state, reflectivity, *far[3:]),
                 "body",
                 specs=[VMEM] * 3 + [HBM] * 2,
                 scratch=[fields, pltpu.SemaphoreType.DMA((2,))],
             )
         else:
-            (acc,) = call(body_next, (sums,), (scal, first, *second, reflectivity, weights), "body", scratch=[fields])
+            (acc,) = call(body_next, (sums,), (first, *second, reflectivity, weights), "body", scratch=[fields])
         *own, other = call(
             halo_dots,
-            (bf(columns - STEP_ROWS, wide), bf(STEP_ROWS, wide), bf(columns, wide)),
-            (scal, h1, h2, acc, weights),
+            (bf(columns - STEP_ROWS[tick], wide), bf(STEP_ROWS[tick], wide), bf(columns, wide)),
+            (h1, h2, acc, weights),
             "edges",
         )
         first = lax.ppermute(other, "depth", SECOND)
@@ -271,7 +265,7 @@
         got_direct = lax.ppermute(own[0], "depth", FIRST_DIRECT)
         got_forward = lax.ppermute(got_step, "depth", FIRST_FORWARD)
         second = (*own, got_direct, got_step, got_forward)
-    return call(finish, (bf(1, columns, wide),) * 2, (scal, first, *second), "finish")
+    return call(finish, (bf(1, columns, wide),) * 2, (first, *second), "finish")
 
 
 def solution(mesh):

time: 188 us -> 180 us (0.957)
  Pallas kernels: 29.2 us -> 22 us
  starting transfers between devices: 62.7 us -> 59.5 us
  waiting for transfers between devices: 94.4 us -> 97.4 us
    ppermute x4, waiting for transfers between devices: 44.8 us -> 29 us  [on_device(): got_forward = lax.ppermute(got_step, 'depth', FIRST_FORWARD)]
    ppermute x4, waiting for transfers between devices: 37 us -> 51.3 us  [on_device(): got_direct = lax.ppermute(own[0], 'depth', FIRST_DIRECT)]
    pallas_call x13, Pallas kernels: 29.2 us -> 22 us  [call(): pl.pallas_call(kernel, out_shape=tuple(outs), in_specs=specs or [VMEM] *...]
    ppermute x4, starting transfers between devices: 33.8 us -> 26.8 us  [on_device(): got_direct = lax.ppermute(own[0], 'depth', FIRST_DIRECT)]
    ppermute x4, starting transfers between devices: 6.84 us -> 9.9 us  [on_device(): h1 = lax.ppermute(e1, 'lat', inside)]
    ppermute x4, waiting for transfers between devices: 0.01 us -> 2.99 us  [on_device(): got_step = lax.ppermute(own[1], 'depth', FIRST_STEP)]
  transfers between devices with their start and end apart: 24 -> 24, of which waited for: 11 -> 12; matrix products, arithmetic and copies ran while one was open for 0% -> 0% of each run, Pallas kernels for 8% -> 7%
where the time goes in v3:
time: 180 us
  waiting for transfers between devices  97.4 us (54%)
  starting transfers between devices  59.5 us (33%)
  Pallas kernels  22 us (12%)
    ppermute x4, waiting for transfers between devices, on_device(): got_direct = lax.ppermute(own[0], 'depth', FIRST_DIRECT)  51.3 us
    ppermute x4, waiting for transfers between devices, on_device(): got_forward = lax.ppermute(got_step, 'depth', FIRST_FORWARD)  29 us
    ppermute x4, starting transfers between devices, on_device(): got_direct = lax.ppermute(own[0], 'depth', FIRST_DIRECT)  26.8 us
    pallas_call x13, Pallas kernels, call(): pl.pallas_call(kernel, out_shape=tuple(outs), in_specs=specs or [VMEM] *...  22 us
    ppermute x4, waiting for transfers between devices, on_device(): h2 = lax.ppermute(e2, 'lat', outside)  14.1 us
    ppermute x4, starting transfers between devices, on_device(): h2 = lax.ppermute(e2, 'lat', outside)  10.2 us
    ppermute x4, starting transfers between devices, on_device(): h1 = lax.ppermute(e1, 'lat', inside)  9.9 us
    ppermute x4, starting transfers between devices, on_device(): got_step = lax.ppermute(own[1], 'depth', FIRST_STEP)  6.61 us
  transfers between devices with their start and end apart: 24, of which 12 were waited for; matrix products, arithmetic and copies ran while one was open for 0% of the time, Pallas kernels for 7%

profile of v3, /device:TPU:57, one launch (start us, length us, event | category | flops | bytes accessed | tf_op | source)
XLA Modules:
  0.0 179.8 jit_solution(1402587061023626601)
XLA Ops:
  0.7 1.9 %ends.4 = (bf16[2,192,512]{2,1,0:T(8,128)(2,1)S(1)}, bf16[2,192,512]{2,1,0:T(8,128)(2,1)S(1)}) custom-call(bf16[1,192,2048]{2,1,0:T(8,128)(2,1)} %refs_0_.3, bf16[1,192,2048]{2,1,0:T(8,128)(2,1)} %refs_1_.3, f32[1,2048]{1,0:T(1,128)} %refs_6_.11), custom_call_target="tpu_custom_call" | custom-call | flops 10000000000 | bytes 1 | tf_op jit(solution)/shard_map/ends/pallas_call | solution.py:44
  3.4 3.0 %collective-permute-start.1 = (bf16[2,192,512]{2,1,0:T(8,128)(2,1)S(1)}, bf16[2,192,512]{2,1,0:T(8,128)(2,1)S(1)}, u32[]{:S(2)}, u32[]{:S(2)}) collective-permute-start(bf16[2,192,512]{2,1,0:T(8,128)(2,1)S(1)} %get-tuple-element.25), channel_id=1, source_target_pairs={{1,2},{2,1},{3,4},{4,3},{5,6},{6,5},{7,8},{8,7},{9,10},{10,9},{11,... | collective-permute-start | bytes 1179656 | tf_op jit(solution)/shard_map/ppermute | solution.py:244
  6.4 5.0 %body.4 = (f32[2,384,1024]{2,1,0:T(8,128)S(1)}, bf16[2,2048,1024]{2,1,0:T(8,128)(2,1)S(1)}) custom-call(bf16[1,192,2048]{2,1,0:T(8,128)(2,1)S(1)} %copy-done, bf16[1,192,2048]{2,1,0:T(8,128)(2,1)S(1)} %copy-done.1, f32[1,2048]{1,0:T(1,128)S(1)} %copy-done.2, bf16[1,1,2048,1024]{3,2,1,0:T(8,128)(2,1)} %refs_3_.1, bf16[1,1,2048,1024]{3,2,1,0:T(8,128)(2,1)} %refs_4_.1), custom_call_target="tpu_custom_call" | custom-call | flops 10000000000 | bytes 1 | tf_op jit(solution)/shard_map/body/pallas_call | solution.py:44
  11.4 1.3 collective-permute-done.1.refs_1_
  14.3 2.7 %collective-permute-start.4 = (bf16[80,2048]{1,0:T(8,128)(2,1)S(1)}, bf16[80,2048]{1,0:T(8,128)(2,1)S(1)}, u32[]{:S(2)}, u32[]{:S(2)}) collective-permute-start(bf16[80,2048]{1,0:T(8,128)(2,1)S(1)} %get-tuple-element.30.refs_2_), channel_id=1, source_target_pairs={{32,64},{64,32},{160,192},{192,160},{96,0},{128,224},{33,65},{65,3... | collective-permute-start | bytes 983048 | tf_op jit(solution)/shard_map/ppermute | solution.py:264
  17.0 9.5 %collective-permute-start.3 = (bf16[112,2048]{1,0:T(8,128)(2,1)S(1)}, bf16[112,2048]{1,0:T(8,128)(2,1)S(1)}, u32[]{:S(2)}, u32[]{:S(2)}) collective-permute-start(bf16[112,2048]{1,0:T(8,128)(2,1)S(1)} %get-tuple-element.29.refs_1_), channel_id=1, source_target_pairs={{32,64},{64,32},{160,192},{192,160},{96,128},{128,96},{33,65},{65,... | collective-permute-start | bytes 1376264 | tf_op jit(solution)/shard_map/ppermute | solution.py:265
  27.9 17.8 %collective-permute-done.3.refs_3_ = bf16[112,2048]{1,0:T(8,128)(2,1)S(1)} collective-permute-done((bf16[112,2048]{1,0:T(8,128)(2,1)S(1)}, bf16[112,2048]{1,0:T(8,128)(2,1)S(1)}, u32[]{:S(2)}, u32[]{:S(2)}) %collective-permute-start.3) | collective-permute-done | bytes 458784 | tf_op jit(solution)/shard_map/ppermute | solution.py:265
  45.7 2.4 %collective-permute-done.5.refs_5_ = bf16[80,2048]{1,0:T(8,128)(2,1)S(1)} collective-permute-done((bf16[80,2048]{1,0:T(8,128)(2,1)S(1)}, bf16[80,2048]{1,0:T(8,128)(2,1)S(1)}, u32[]{:S(2)}, u32[]{:S(2)}) %collective-permute-start.5) | collective-permute-done | bytes 327712 | tf_op jit(solution)/shard_map/ppermute | solution.py:266
  48.6 1.6 collective-permute-start.6
  50.1 2.7 %collective-permute-start.7 = (bf16[2,192,512]{2,1,0:T(8,128)(2,1)S(1)}, bf16[2,192,512]{2,1,0:T(8,128)(2,1)S(1)}, u32[]{:S(2)}, u32[]{:S(2)}) collective-permute-start(bf16[2,192,512]{2,1,0:T(8,128)(2,1)S(1)} %get-tuple-element.32), channel_id=1, source_target_pairs={{1,2},{2,1},{3,4},{4,3},{5,6},{6,5},{7,8},{8,7},{9,10},{10,9},{11,... | collective-permute-start | bytes 1179656 | tf_op jit(solution)/shard_map/ppermute | solution.py:244
  52.8 2.7 %body.5.refs_2_ = f32[2,384,1024]{2,1,0:T(8,128)S(1)} custom-call(bf16[192,2048]{1,0:T(8,128)(2,1)S(1)} %collective-permute-done.2.refs_0_, bf16[112,2048]{1,0:T(8,128)(2,1)S(1)} %get-tuple-element.29.refs_1_, bf16[80,2048]{1,0:T(8,128)(2,1)S(1)} %get-tuple-element.30.refs_2_, bf16[112,2048]{1,0:T(8,128)(2,1)S(1)} %collective-permute-done.3.refs_3_, ...), custom_call_target="tpu_custom_call" | custom-call | flops 10000000000 | bytes 1 | tf_op jit(solution)/shard_map/body/pallas_call | solution.py:44
  55.5 4.0 %collective-permute-done.7.refs_1_ = bf16[2,192,512]{2,1,0:T(8,128)(2,1)S(1)} collective-permute-done((bf16[2,192,512]{2,1,0:T(8,128)(2,1)S(1)}, bf16[2,192,512]{2,1,0:T(8,128)(2,1)S(1)}, u32[]{:S(2)}, u32[]{:S(2)}) %collective-permute-start.7) | collective-permute-done | bytes 393248 | tf_op jit(solution)/shard_map/ppermute | solution.py:244
  60.7 1.3 collective-permute-start.10
  62.0 7.7 %collective-permute-start.9 = (bf16[128,2048]{1,0:T(8,128)(2,1)S(1)}, bf16[128,2048]{1,0:T(8,128)(2,1)S(1)}, u32[]{:S(2)}, u32[]{:S(2)}) collective-permute-start(bf16[128,2048]{1,0:T(8,128)(2,1)S(1)} %get-tuple-element.34.refs_1_), channel_id=1, source_target_pairs={{32,64},{64,32},{160,192},{192,160},{96,128},{128,96},{33,65},{65,... | collective-permute-start | bytes 1572872 | tf_op jit(solution)/shard_map/ppermute | solution.py:265
  71.0 16.4 %collective-permute-done.11.refs_5_ = bf16[64,2048]{1,0:T(8,128)(2,1)S(1)} collective-permute-done((bf16[64,2048]{1,0:T(8,128)(2,1)S(1)}, bf16[64,2048]{1,0:T(8,128)(2,1)S(1)}, u32[]{:S(2)}, u32[]{:S(2)}) %collective-permute-start.11) | collective-permute-done | bytes 262176 | tf_op jit(solution)/shard_map/ppermute | solution.py:266
  87.4 7.3 %collective-permute-done.9.refs_3_ = bf16[128,2048]{1,0:T(8,128)(2,1)S(1)} collective-permute-done((bf16[128,2048]{1,0:T(8,128)(2,1)S(1)}, bf16[128,2048]{1,0:T(8,128)(2,1)S(1)}, u32[]{:S(2)}, u32[]{:S(2)}) %collective-permute-start.9) | collective-permute-done | bytes 524320 | tf_op jit(solution)/shard_map/ppermute | solution.py:265
  96.1 2.6 %collective-permute-start.13 = (bf16[2,192,512]{2,1,0:T(8,128)(2,1)S(1)}, bf16[2,192,512]{2,1,0:T(8,128)(2,1)S(1)}, u32[]{:S(2)}, u32[]{:S(2)}) collective-permute-start(bf16[2,192,512]{2,1,0:T(8,128)(2,1)S(1)} %get-tuple-element.37), channel_id=1, source_target_pairs={{1,2},{2,1},{3,4},{4,3},{5,6},{6,5},{7,8},{8,7},{9,10},{10,9},{11,... | collective-permute-start | bytes 1179656 | tf_op jit(solution)/shard_map/ppermute | solution.py:244
  98.6 2.7 %body.6.refs_2_ = f32[2,384,1024]{2,1,0:T(8,128)S(1)} custom-call(bf16[192,2048]{1,0:T(8,128)(2,1)S(1)} %collective-permute-done.8.refs_0_, bf16[128,2048]{1,0:T(8,128)(2,1)S(1)} %get-tuple-element.34.refs_1_, bf16[64,2048]{1,0:T(8,128)(2,1)S(1)} %get-tuple-element.35.refs_2_, bf16[128,2048]{1,0:T(8,128)(2,1)S(1)} %collective-permute-done.9.refs_3_, ...), custom_call_target="tpu_custom_call" | custom-call | flops 10000000000 | bytes 1 | tf_op jit(solution)/shard_map/body/pallas_call | solution.py:44
  101.3 4.1 %collective-permute-done.13.refs_1_ = bf16[2,192,512]{2,1,0:T(8,128)(2,1)S(1)} collective-permute-done((bf16[2,192,512]{2,1,0:T(8,128)(2,1)S(1)}, bf16[2,192,512]{2,1,0:T(8,128)(2,1)S(1)}, u32[]{:S(2)}, u32[]{:S(2)}) %collective-permute-start.13) | collective-permute-done | bytes 393248 | tf_op jit(solution)/shard_map/ppermute | solution.py:244
  106.6 1.3 collective-permute-start.16
  107.9 7.2 %collective-permute-start.15 = (bf16[128,2048]{1,0:T(8,128)(2,1)S(1)}, bf16[128,2048]{1,0:T(8,128)(2,1)S(1)}, u32[]{:S(2)}, u32[]{:S(2)}) collective-permute-start(bf16[128,2048]{1,0:T(8,128)(2,1)S(1)} %get-tuple-element.39.refs_1_), channel_id=1, source_target_pairs={{32,64},{64,32},{160,192},{192,160},{96,128},{128,96},{33,65},{65,... | collective-permute-start | bytes 1572872 | tf_op jit(solution)/shard_map/ppermute | solution.py:265
  116.4 10.2 %collective-permute-done.17.refs_5_ = bf16[64,2048]{1,0:T(8,128)(2,1)S(1)} collective-permute-done((bf16[64,2048]{1,0:T(8,128)(2,1)S(1)}, bf16[64,2048]{1,0:T(8,128)(2,1)S(1)}, u32[]{:S(2)}, u32[]{:S(2)}) %collective-permute-start.17) | collective-permute-done | bytes 262176 | tf_op jit(solution)/shard_map/ppermute | solution.py:266
  126.6 2.7 %collective-permute-done.15.refs_3_ = bf16[128,2048]{1,0:T(8,128)(2,1)S(1)} collective-permute-done((bf16[128,2048]{1,0:T(8,128)(2,1)S(1)}, bf16[128,2048]{1,0:T(8,128)(2,1)S(1)}, u32[]{:S(2)}, u32[]{:S(2)}) %collective-permute-start.15) | collective-permute-done | bytes 524320 | tf_op jit(solution)/shard_map/ppermute | solution.py:265
  129.8 6.7 %collective-permute-start.18 = (bf16[2,192,512]{2,1,0:T(8,128)(2,1)S(1)}, bf16[2,192,512]{2,1,0:T(8,128)(2,1)S(1)}, u32[]{:S(2)}, u32[]{:S(2)}) collective-permute-start(bf16[2,192,512]{2,1,0:T(8,128)(2,1)S(1)} %get-tuple-element.41), channel_id=1, source_target_pairs={{0,1},{1,0},{2,3},{3,2},{4,5},{5,4},{6,7},{7,6},{8,9},{9,8},{10,11... | collective-permute-start | bytes 1179656 | tf_op jit(solution)/shard_map/ppermute | solution.py:245
  136.5 1.9 %collective-permute-start.19 = (bf16[2,192,512]{2,1,0:T(8,128)(2,1)S(1)}, bf16[2,192,512]{2,1,0:T(8,128)(2,1)S(1)}, u32[]{:S(2)}, u32[]{:S(2)}) collective-permute-start(bf16[2,192,512]{2,1,0:T(8,128)(2,1)S(1)} %get-tuple-element.42), channel_id=1, source_target_pairs={{1,2},{2,1},{3,4},{4,3},{5,6},{6,5},{7,8},{8,7},{9,10},{10,9},{11,... | collective-permute-start | bytes 1179656 | tf_op jit(solution)/shard_map/ppermute | solution.py:244
  138.4 2.7 %body.7.refs_2_ = f32[2,384,1024]{2,1,0:T(8,128)S(1)} custom-call(bf16[192,2048]{1,0:T(8,128)(2,1)S(1)} %collective-permute-done.14.refs_0_, bf16[128,2048]{1,0:T(8,128)(2,1)S(1)} %get-tuple-element.39.refs_1_, bf16[64,2048]{1,0:T(8,128)(2,1)S(1)} %get-tuple-element.40.refs_2_, bf16[128,2048]{1,0:T(8,128)(2,1)S(1)} %collective-permute-done.15.refs_3_, ...), custom_call_target="tpu_custom_call" | custom-call | flops 10000000000 | bytes 1 | tf_op jit(solution)/shard_map/body/pallas_call | solution.py:44
  141.1 4.8 %collective-permute-done.19.refs_1_ = bf16[2,192,512]{2,1,0:T(8,128)(2,1)S(1)} collective-permute-done((bf16[2,192,512]{2,1,0:T(8,128)(2,1)S(1)}, bf16[2,192,512]{2,1,0:T(8,128)(2,1)S(1)}, u32[]{:S(2)}, u32[]{:S(2)}) %collective-permute-start.19) | collective-permute-done | bytes 393248 | tf_op jit(solution)/shard_map/ppermute | solution.py:244
  147.1 1.3 collective-permute-start.22
  148.4 2.3 %collective-permute-start.21 = (bf16[112,2048]{1,0:T(8,128)(2,1)S(1)}, bf16[112,2048]{1,0:T(8,128)(2,1)S(1)}, u32[]{:S(2)}, u32[]{:S(2)}) collective-permute-start(bf16[112,2048]{1,0:T(8,128)(2,1)S(1)} %get-tuple-element.44.refs_1_), channel_id=1, source_target_pairs={{32,64},{64,32},{160,192},{192,160},{96,128},{128,96},{33,65},{65,... | collective-permute-start | bytes 1376264 | tf_op jit(solution)/shard_map/ppermute | solution.py:265
  150.7 3.0 %collective-permute-done.22.refs_4_ = bf16[80,2048]{1,0:T(8,128)(2,1)S(1)} collective-permute-done((bf16[80,2048]{1,0:T(8,128)(2,1)S(1)}, bf16[80,2048]{1,0:T(8,128)(2,1)S(1)}, u32[]{:S(2)}, u32[]{:S(2)}) %collective-permute-start.22) | collective-permute-done | bytes 327712 | tf_op jit(solution)/shard_map/ppermute | solution.py:264
  155.0 23.5 %collective-permute-done.21.refs_3_ = bf16[112,2048]{1,0:T(8,128)(2,1)S(1)} collective-permute-done((bf16[112,2048]{1,0:T(8,128)(2,1)S(1)}, bf16[112,2048]{1,0:T(8,128)(2,1)S(1)}, u32[]{:S(2)}, u32[]{:S(2)}) %collective-permute-start.21) | collective-permute-done | bytes 458784 | tf_op jit(solution)/shard_map/ppermute | solution.py:265
  178.5 1.3 finish.1
  (35 shorter events, 13.3 us)
Async XLA Ops:
  0.6 5.8 %copy-start.2 = (f32[1,2048]{1,0:T(1,128)S(1)}, f32[1,2048]{1,0:T(1,128)}, u32[]{:S(2)}) copy-start(f32[1,2048]{1,0:T(1,128)} %refs_6_.11) | copy-start | bytes 24580
  0.6 5.8 %copy-start.1 = (bf16[1,192,2048]{2,1,0:T(8,128)(2,1)S(1)}, bf16[1,192,2048]{2,1,0:T(8,128)(2,1)}, u32[]{:S(2)}) copy-start(bf16[1,192,2048]{2,1,0:T(8,128)(2,1)} %refs_1_.3) | copy-start | bytes 2359300
  0.6 5.8 %copy-start = (bf16[1,192,2048]{2,1,0:T(8,128)(2,1)S(1)}, bf16[1,192,2048]{2,1,0:T(8,128)(2,1)}, u32[]{:S(2)}) copy-start(bf16[1,192,2048]{2,1,0:T(8,128)(2,1)} %refs_0_.3) | copy-start | bytes 2359300
  2.6 8.8 %collective-permute-start = (bf16[2,192,512]{2,1,0:T(8,128)(2,1)S(1)}, bf16[2,192,512]{2,1,0:T(8,128)(2,1)S(1)}, u32[]{:S(2)}, u32[]{:S(2)}) collective-permute-start(bf16[2,192,512]{2,1,0:T(8,128)(2,1)S(1)} %get-tuple-element.24), channel_id=1, source_target_pairs={{0,1},{1,0},{2,3},{3,2},{4,5},{5,4},{6,7},{7,6},{8,9},{9,8},{10,11... | collective-permute-start | bytes 1179656 | tf_op jit(solution)/shard_map/ppermute | solution.py:245
  3.4 9.4 %collective-permute-start.1 = (bf16[2,192,512]{2,1,0:T(8,128)(2,1)S(1)}, bf16[2,192,512]{2,1,0:T(8,128)(2,1)S(1)}, u32[]{:S(2)}, u32[]{:S(2)}) collective-permute-start(bf16[2,192,512]{2,1,0:T(8,128)(2,1)S(1)} %get-tuple-element.25), channel_id=1, source_target_pairs={{1,2},{2,1},{3,4},{4,3},{5,6},{6,5},{7,8},{8,7},{9,10},{10,9},{11,... | collective-permute-start | bytes 1179656 | tf_op jit(solution)/shard_map/ppermute | solution.py:244
  13.8 34.3 %collective-permute-start.2 = (bf16[192,2048]{1,0:T(8,128)(2,1)S(1)}, bf16[192,2048]{1,0:T(8,128)(2,1)S(1)}, u32[]{:S(2)}, u32[]{:S(2)}) collective-permute-start(bf16[192,2048]{1,0:T(8,128)(2,1)S(1)} %get-tuple-element.28), channel_id=1, source_target_pairs={{0,32},{32,0},{64,96},{96,64},{128,160},{160,128},{192,224},{224,1... | collective-permute-start | bytes 2359304 | tf_op jit(solution)/shard_map/ppermute | solution.py:263
  14.3 12.2 %collective-permute-start.4 = (bf16[80,2048]{1,0:T(8,128)(2,1)S(1)}, bf16[80,2048]{1,0:T(8,128)(2,1)S(1)}, u32[]{:S(2)}, u32[]{:S(2)}) collective-permute-start(bf16[80,2048]{1,0:T(8,128)(2,1)S(1)} %get-tuple-element.30.refs_2_), channel_id=1, source_target_pairs={{32,64},{64,32},{160,192},{192,160},{96,0},{128,224},{33,65},{65,3... | collective-permute-start | bytes 983048 | tf_op jit(solution)/shard_map/ppermute | solution.py:264
  17.0 28.6 %collective-permute-start.3 = (bf16[112,2048]{1,0:T(8,128)(2,1)S(1)}, bf16[112,2048]{1,0:T(8,128)(2,1)S(1)}, u32[]{:S(2)}, u32[]{:S(2)}) collective-permute-start(bf16[112,2048]{1,0:T(8,128)(2,1)S(1)} %get-tuple-element.29.refs_1_), channel_id=1, source_target_pairs={{32,64},{64,32},{160,192},{192,160},{96,128},{128,96},{33,65},{65,... | collective-permute-start | bytes 1376264 | tf_op jit(solution)/shard_map/ppermute | solution.py:265
  26.6 21.5 %collective-permute-start.5 = (bf16[80,2048]{1,0:T(8,128)(2,1)S(1)}, bf16[80,2048]{1,0:T(8,128)(2,1)S(1)}, u32[]{:S(2)}, u32[]{:S(2)}) collective-permute-start(bf16[80,2048]{1,0:T(8,128)(2,1)S(1)} %collective-permute-done.4.refs_4_), channel_id=1, source_target_pairs={{0,128},{224,96},{1,129},{225,97},{2,130},{226,98},{3,131},{227,99... | collective-permute-start | bytes 983048 | tf_op jit(solution)/shard_map/ppermute | solution.py:266
  48.6 7.0 %collective-permute-start.6 = (bf16[2,192,512]{2,1,0:T(8,128)(2,1)S(1)}, bf16[2,192,512]{2,1,0:T(8,128)(2,1)S(1)}, u32[]{:S(2)}, u32[]{:S(2)}) collective-permute-start(bf16[2,192,512]{2,1,0:T(8,128)(2,1)S(1)} %get-tuple-element.31), channel_id=1, source_target_pairs={{0,1},{1,0},{2,3},{3,2},{4,5},{5,4},{6,7},{7,6},{8,9},{9,8},{10,11... | collective-permute-start | bytes 1179656 | tf_op jit(solution)/shard_map/ppermute | solution.py:245
  50.1 9.4 %collective-permute-start.7 = (bf16[2,192,512]{2,1,0:T(8,128)(2,1)S(1)}, bf16[2,192,512]{2,1,0:T(8,128)(2,1)S(1)}, u32[]{:S(2)}, u32[]{:S(2)}) collective-permute-start(bf16[2,192,512]{2,1,0:T(8,128)(2,1)S(1)} %get-tuple-element.32), channel_id=1, source_target_pairs={{1,2},{2,1},{3,4},{4,3},{5,6},{6,5},{7,8},{8,7},{9,10},{10,9},{11,... | collective-permute-start | bytes 1179656 | tf_op jit(solution)/shard_map/ppermute | solution.py:244
  60.6 34.2 %collective-permute-start.8 = (bf16[192,2048]{1,0:T(8,128)(2,1)S(1)}, bf16[192,2048]{1,0:T(8,128)(2,1)S(1)}, u32[]{:S(2)}, u32[]{:S(2)}) collective-permute-start(bf16[192,2048]{1,0:T(8,128)(2,1)S(1)} %get-tuple-element.33), channel_id=1, source_target_pairs={{0,32},{32,0},{64,96},{96,64},{128,160},{160,128},{192,224},{224,1... | collective-permute-start | bytes 2359304 | tf_op jit(solution)/shard_map/ppermute | solution.py:263
  60.7 9.0 %collective-permute-start.10 = (bf16[64,2048]{1,0:T(8,128)(2,1)S(1)}, bf16[64,2048]{1,0:T(8,128)(2,1)S(1)}, u32[]{:S(2)}, u32[]{:S(2)}) collective-permute-start(bf16[64,2048]{1,0:T(8,128)(2,1)S(1)} %get-tuple-element.35.refs_2_), channel_id=1, source_target_pairs={{32,64},{64,32},{160,192},{192,160},{96,0},{128,224},{33,65},{65,3... | collective-permute-start | bytes 786440 | tf_op jit(solution)/shard_map/ppermute | solution.py:264
  62.0 32.8 %collective-permute-start.9 = (bf16[128,2048]{1,0:T(8,128)(2,1)S(1)}, bf16[128,2048]{1,0:T(8,128)(2,1)S(1)}, u32[]{:S(2)}, u32[]{:S(2)}) collective-permute-start(bf16[128,2048]{1,0:T(8,128)(2,1)S(1)} %get-tuple-element.34.refs_1_), channel_id=1, source_target_pairs={{32,64},{64,32},{160,192},{192,160},{96,128},{128,96},{33,65},{65,... | collective-permute-start | bytes 1572872 | tf_op jit(solution)/shard_map/ppermute | solution.py:265
  69.7 17.7 %collective-permute-start.11 = (bf16[64,2048]{1,0:T(8,128)(2,1)S(1)}, bf16[64,2048]{1,0:T(8,128)(2,1)S(1)}, u32[]{:S(2)}, u32[]{:S(2)}) collective-permute-start(bf16[64,2048]{1,0:T(8,128)(2,1)S(1)} %collective-permute-done.10.refs_4_), channel_id=1, source_target_pairs={{0,128},{224,96},{1,129},{225,97},{2,130},{226,98},{3,131},{227,99... | collective-permute-start | bytes 786440 | tf_op jit(solution)/shard_map/ppermute | solution.py:266
  95.2 6.1 %collective-permute-start.12 = (bf16[2,192,512]{2,1,0:T(8,128)(2,1)S(1)}, bf16[2,192,512]{2,1,0:T(8,128)(2,1)S(1)}, u32[]{:S(2)}, u32[]{:S(2)}) collective-permute-start(bf16[2,192,512]{2,1,0:T(8,128)(2,1)S(1)} %get-tuple-element.36), channel_id=1, source_target_pairs={{0,1},{1,0},{2,3},{3,2},{4,5},{5,4},{6,7},{7,6},{8,9},{9,8},{10,11... | collective-permute-start | bytes 1179656 | tf_op jit(solution)/shard_map/ppermute | solution.py:245
  96.1 9.4 %collective-permute-start.13 = (bf16[2,192,512]{2,1,0:T(8,128)(2,1)S(1)}, bf16[2,192,512]{2,1,0:T(8,128)(2,1)S(1)}, u32[]{:S(2)}, u32[]{:S(2)}) collective-permute-start(bf16[2,192,512]{2,1,0:T(8,128)(2,1)S(1)} %get-tuple-element.37), channel_id=1, source_target_pairs={{1,2},{2,1},{3,4},{4,3},{5,6},{6,5},{7,8},{8,7},{9,10},{10,9},{11,... | collective-permute-start | bytes 1179656 | tf_op jit(solution)/shard_map/ppermute | solution.py:244
  106.5 22.8 %collective-permute-start.14 = (bf16[192,2048]{1,0:T(8,128)(2,1)S(1)}, bf16[192,2048]{1,0:T(8,128)(2,1)S(1)}, u32[]{:S(2)}, u32[]{:S(2)}) collective-permute-start(bf16[192,2048]{1,0:T(8,128)(2,1)S(1)} %get-tuple-element.38), channel_id=1, source_target_pairs={{0,32},{32,0},{64,96},{96,64},{128,160},{160,128},{192,224},{224,1... | collective-permute-start | bytes 2359304 | tf_op jit(solution)/shard_map/ppermute | solution.py:263
  106.6 8.5 %collective-permute-start.16 = (bf16[64,2048]{1,0:T(8,128)(2,1)S(1)}, bf16[64,2048]{1,0:T(8,128)(2,1)S(1)}, u32[]{:S(2)}, u32[]{:S(2)}) collective-permute-start(bf16[64,2048]{1,0:T(8,128)(2,1)S(1)} %get-tuple-element.40.refs_2_), channel_id=1, source_target_pairs={{32,64},{64,32},{160,192},{192,160},{96,0},{128,224},{33,65},{65,3... | collective-permute-start | bytes 786440 | tf_op jit(solution)/shard_map/ppermute | solution.py:264
  107.9 21.4 %collective-permute-start.15 = (bf16[128,2048]{1,0:T(8,128)(2,1)S(1)}, bf16[128,2048]{1,0:T(8,128)(2,1)S(1)}, u32[]{:S(2)}, u32[]{:S(2)}) collective-permute-start(bf16[128,2048]{1,0:T(8,128)(2,1)S(1)} %get-tuple-element.39.refs_1_), channel_id=1, source_target_pairs={{32,64},{64,32},{160,192},{192,160},{96,128},{128,96},{33,65},{65,... | collective-permute-start | bytes 1572872 | tf_op jit(solution)/shard_map/ppermute | solution.py:265
  115.1 11.5 %collective-permute-start.17 = (bf16[64,2048]{1,0:T(8,128)(2,1)S(1)}, bf16[64,2048]{1,0:T(8,128)(2,1)S(1)}, u32[]{:S(2)}, u32[]{:S(2)}) collective-permute-start(bf16[64,2048]{1,0:T(8,128)(2,1)S(1)} %collective-permute-done.16.refs_4_), channel_id=1, source_target_pairs={{0,128},{224,96},{1,129},{225,97},{2,130},{226,98},{3,131},{227,99... | collective-permute-start | bytes 786440 | tf_op jit(solution)/shard_map/ppermute | solution.py:266
  129.8 11.3 %collective-permute-start.18 = (bf16[2,192,512]{2,1,0:T(8,128)(2,1)S(1)}, bf16[2,192,512]{2,1,0:T(8,128)(2,1)S(1)}, u32[]{:S(2)}, u32[]{:S(2)}) collective-permute-start(bf16[2,192,512]{2,1,0:T(8,128)(2,1)S(1)} %get-tuple-element.41), channel_id=1, source_target_pairs={{0,1},{1,0},{2,3},{3,2},{4,5},{5,4},{6,7},{7,6},{8,9},{9,8},{10,11... | collective-permute-start | bytes 1179656 | tf_op jit(solution)/shard_map/ppermute | solution.py:245
  136.5 9.4 %collective-permute-start.19 = (bf16[2,192,512]{2,1,0:T(8,128)(2,1)S(1)}, bf16[2,192,512]{2,1,0:T(8,128)(2,1)S(1)}, u32[]{:S(2)}, u32[]{:S(2)}) collective-permute-start(bf16[2,192,512]{2,1,0:T(8,128)(2,1)S(1)} %get-tuple-element.42), channel_id=1, source_target_pairs={{1,2},{2,1},{3,4},{4,3},{5,6},{6,5},{7,8},{8,7},{9,10},{10,9},{11,... | collective-permute-start | bytes 1179656 | tf_op jit(solution)/shard_map/ppermute | solution.py:244
  147.0 31.6 %collective-permute-start.20 = (bf16[192,2048]{1,0:T(8,128)(2,1)S(1)}, bf16[192,2048]{1,0:T(8,128)(2,1)S(1)}, u32[]{:S(2)}, u32[]{:S(2)}) collective-permute-start(bf16[192,2048]{1,0:T(8,128)(2,1)S(1)} %get-tuple-element.43), channel_id=1, source_target_pairs={{0,32},{32,0},{64,96},{96,64},{128,160},{160,128},{192,224},{224,1... | collective-permute-start | bytes 2359304 | tf_op jit(solution)/shard_map/ppermute | solution.py:263
  147.1 6.7 %collective-permute-start.22 = (bf16[80,2048]{1,0:T(8,128)(2,1)S(1)}, bf16[80,2048]{1,0:T(8,128)(2,1)S(1)}, u32[]{:S(2)}, u32[]{:S(2)}) collective-permute-start(bf16[80,2048]{1,0:T(8,128)(2,1)S(1)} %get-tuple-element.45.refs_2_), channel_id=1, source_target_pairs={{32,64},{64,32},{160,192},{192,160},{96,0},{128,224},{33,65},{65,3... | collective-permute-start | bytes 983048 | tf_op jit(solution)/shard_map/ppermute | solution.py:264
  148.4 30.1 %collective-permute-start.21 = (bf16[112,2048]{1,0:T(8,128)(2,1)S(1)}, bf16[112,2048]{1,0:T(8,128)(2,1)S(1)}, u32[]{:S(2)}, u32[]{:S(2)}) collective-permute-start(bf16[112,2048]{1,0:T(8,128)(2,1)S(1)} %get-tuple-element.44.refs_1_), channel_id=1, source_target_pairs={{32,64},{64,32},{160,192},{192,160},{96,128},{128,96},{33,65},{65,... | collective-permute-start | bytes 1376264 | tf_op jit(solution)/shard_map/ppermute | solution.py:265
  153.7 24.8 %collective-permute-start.23 = (bf16[80,2048]{1,0:T(8,128)(2,1)S(1)}, bf16[80,2048]{1,0:T(8,128)(2,1)S(1)}, u32[]{:S(2)}, u32[]{:S(2)}) collective-permute-start(bf16[80,2048]{1,0:T(8,128)(2,1)S(1)} %collective-permute-done.22.refs_4_), channel_id=1, source_target_pairs={{0,128},{224,96},{1,129},{225,97},{2,130},{226,98},{3,131},{227,99... | collective-permute-start | bytes 983048 | tf_op jit(solution)/shard_map/ppermute | solution.py:266

commit v4 on v3

--- a/solution.py
+++ b/solution.py
@@ -23,7 +23,7 @@
 
 INNER = swap((1, 2), (5, 6))
 FIRST_DIRECT = INNER + swap((3, 4))
-FIRST_STEP = INNER + [(3, 0), (4, 7)]
+FIRST_STEP = INNER + swap((0, 3), (4, 7))
 FIRST_FORWARD = [(0, 4), (7, 3)]
 SECOND = swap((0, 1), (2, 3), (4, 5), (6, 7))
 

time: 180 us -> 187 us (1.039)
  the two profiles are of different devices: /device:TPU:57 before, /device:TPU:7 now
where the time goes in v4:
time: 187 us
  waiting for transfers between devices  103 us (55%)
  starting transfers between devices  60.1 us (32%)
  Pallas kernels  22.1 us (12%)
    ppermute x4, waiting for transfers between devices, on_device(): got_forward = lax.ppermute(got_step, 'depth', FIRST_FORWARD)  51.4 us
    ppermute x4, starting transfers between devices, on_device(): got_forward = lax.ppermute(got_step, 'depth', FIRST_FORWARD)  42.6 us
    ppermute x4, waiting for transfers between devices, on_device(): got_step = lax.ppermute(own[1], 'depth', FIRST_STEP)  29.6 us
    ppermute x4, waiting for transfers between devices, on_device(): h2 = lax.ppermute(e2, 'lat', outside)  22.4 us
    pallas_call x13, Pallas kernels, call(): pl.pallas_call(kernel, out_shape=tuple(outs), in_specs=specs or [VMEM] *...  22.1 us
    ppermute x4, starting transfers between devices, on_device(): h2 = lax.ppermute(e2, 'lat', outside)  9.1 us
  transfers between devices with their start and end apart: 24, of which 12 were waited for; matrix products, arithmetic and copies ran while one was open for 0% of the time, Pallas kernels for 7%

profile of v4, /device:TPU:7, one launch (start us, length us, event | category | flops | bytes accessed | tf_op | source)
XLA Modules:
  0.0 186.6 jit_solution(1142836857165295543)
XLA Ops:
  0.7 1.9 %ends.4 = (bf16[2,192,512]{2,1,0:T(8,128)(2,1)S(1)}, bf16[2,192,512]{2,1,0:T(8,128)(2,1)S(1)}) custom-call(bf16[1,192,2048]{2,1,0:T(8,128)(2,1)} %refs_0_.3, bf16[1,192,2048]{2,1,0:T(8,128)(2,1)} %refs_1_.3, f32[1,2048]{1,0:T(1,128)} %refs_6_.11), custom_call_target="tpu_custom_call" | custom-call | flops 10000000000 | bytes 1 | tf_op jit(solution)/shard_map/ends/pallas_call | solution.py:44
  3.4 3.4 %collective-permute-start.1 = (bf16[2,192,512]{2,1,0:T(8,128)(2,1)S(1)}, bf16[2,192,512]{2,1,0:T(8,128)(2,1)S(1)}, u32[]{:S(2)}, u32[]{:S(2)}) collective-permute-start(bf16[2,192,512]{2,1,0:T(8,128)(2,1)S(1)} %get-tuple-element.25), channel_id=1, source_target_pairs={{1,2},{2,1},{3,4},{4,3},{5,6},{6,5},{7,8},{8,7},{9,10},{10,9},{11,... | collective-permute-start | bytes 1179656 | tf_op jit(solution)/shard_map/ppermute | solution.py:244
  6.8 5.1 %body.4 = (f32[2,384,1024]{2,1,0:T(8,128)S(1)}, bf16[2,2048,1024]{2,1,0:T(8,128)(2,1)S(1)}) custom-call(bf16[1,192,2048]{2,1,0:T(8,128)(2,1)S(1)} %copy-done, bf16[1,192,2048]{2,1,0:T(8,128)(2,1)S(1)} %copy-done.1, f32[1,2048]{1,0:T(1,128)S(1)} %copy-done.2, bf16[1,1,2048,1024]{3,2,1,0:T(8,128)(2,1)} %refs_3_.1, bf16[1,1,2048,1024]{3,2,1,0:T(8,128)(2,1)} %refs_4_.1), custom_call_target="tpu_custom_call" | custom-call | flops 10000000000 | bytes 1 | tf_op jit(solution)/shard_map/body/pallas_call | solution.py:44
  11.9 2.6 %collective-permute-done.1.refs_1_ = bf16[2,192,512]{2,1,0:T(8,128)(2,1)S(1)} collective-permute-done((bf16[2,192,512]{2,1,0:T(8,128)(2,1)S(1)}, bf16[2,192,512]{2,1,0:T(8,128)(2,1)S(1)}, u32[]{:S(2)}, u32[]{:S(2)}) %collective-permute-start.1) | collective-permute-done | bytes 393248 | tf_op jit(solution)/shard_map/ppermute | solution.py:244
  14.6 1.1 edges.4
  15.6 1.4 collective-permute-start.2
  17.0 1.9 %collective-permute-start.4 = (bf16[80,2048]{1,0:T(8,128)(2,1)S(1)}, bf16[80,2048]{1,0:T(8,128)(2,1)S(1)}, u32[]{:S(2)}, u32[]{:S(2)}) collective-permute-start(bf16[80,2048]{1,0:T(8,128)(2,1)S(1)} %get-tuple-element.30.refs_2_), channel_id=1, source_target_pairs={{32,64},{64,32},{160,192},{192,160},{0,96},{96,0},{128,224},{224,1... | collective-permute-start | bytes 983048 | tf_op jit(solution)/shard_map/ppermute | solution.py:264
  19.6 6.7 %collective-permute-done.4.refs_4_ = bf16[80,2048]{1,0:T(8,128)(2,1)S(1)} collective-permute-done((bf16[80,2048]{1,0:T(8,128)(2,1)S(1)}, bf16[80,2048]{1,0:T(8,128)(2,1)S(1)}, u32[]{:S(2)}, u32[]{:S(2)}) %collective-permute-start.4) | collective-permute-done | bytes 327712 | tf_op jit(solution)/shard_map/ppermute | solution.py:264
  26.3 8.8 %collective-permute-start.5 = (bf16[80,2048]{1,0:T(8,128)(2,1)S(1)}, bf16[80,2048]{1,0:T(8,128)(2,1)S(1)}, u32[]{:S(2)}, u32[]{:S(2)}) collective-permute-start(bf16[80,2048]{1,0:T(8,128)(2,1)S(1)} %collective-permute-done.4.refs_4_), channel_id=1, source_target_pairs={{0,128},{224,96},{1,129},{225,97},{2,130},{226,98},{3,131},{227,99... | collective-permute-start | bytes 983048 | tf_op jit(solution)/shard_map/ppermute | solution.py:266
  35.1 17.1 %collective-permute-done.5.refs_5_ = bf16[80,2048]{1,0:T(8,128)(2,1)S(1)} collective-permute-done((bf16[80,2048]{1,0:T(8,128)(2,1)S(1)}, bf16[80,2048]{1,0:T(8,128)(2,1)S(1)}, u32[]{:S(2)}, u32[]{:S(2)}) %collective-permute-start.5) | collective-permute-done | bytes 327712 | tf_op jit(solution)/shard_map/ppermute | solution.py:266
  52.9 1.9 %collective-permute-start.7 = (bf16[2,192,512]{2,1,0:T(8,128)(2,1)S(1)}, bf16[2,192,512]{2,1,0:T(8,128)(2,1)S(1)}, u32[]{:S(2)}, u32[]{:S(2)}) collective-permute-start(bf16[2,192,512]{2,1,0:T(8,128)(2,1)S(1)} %get-tuple-element.32), channel_id=1, source_target_pairs={{1,2},{2,1},{3,4},{4,3},{5,6},{6,5},{7,8},{8,7},{9,10},{10,9},{11,... | collective-permute-start | bytes 1179656 | tf_op jit(solution)/shard_map/ppermute | solution.py:244
  54.8 2.7 %body.5.refs_2_ = f32[2,384,1024]{2,1,0:T(8,128)S(1)} custom-call(bf16[192,2048]{1,0:T(8,128)(2,1)S(1)} %collective-permute-done.2.refs_0_, bf16[112,2048]{1,0:T(8,128)(2,1)S(1)} %get-tuple-element.29.refs_1_, bf16[80,2048]{1,0:T(8,128)(2,1)S(1)} %get-tuple-element.30.refs_2_, bf16[112,2048]{1,0:T(8,128)(2,1)S(1)} %collective-permute-done.3.refs_3_, ...), custom_call_target="tpu_custom_call" | custom-call | flops 10000000000 | bytes 1 | tf_op jit(solution)/shard_map/body/pallas_call | solution.py:44
  57.5 6.6 %collective-permute-done.7.refs_1_ = bf16[2,192,512]{2,1,0:T(8,128)(2,1)S(1)} collective-permute-done((bf16[2,192,512]{2,1,0:T(8,128)(2,1)S(1)}, bf16[2,192,512]{2,1,0:T(8,128)(2,1)S(1)}, u32[]{:S(2)}, u32[]{:S(2)}) %collective-permute-start.7) | collective-permute-done | bytes 393248 | tf_op jit(solution)/shard_map/ppermute | solution.py:244
  64.1 1.1 edges.5
  66.3 7.2 %collective-permute-done.10.refs_4_ = bf16[64,2048]{1,0:T(8,128)(2,1)S(1)} collective-permute-done((bf16[64,2048]{1,0:T(8,128)(2,1)S(1)}, bf16[64,2048]{1,0:T(8,128)(2,1)S(1)}, u32[]{:S(2)}, u32[]{:S(2)}) %collective-permute-start.10) | collective-permute-done | bytes 262176 | tf_op jit(solution)/shard_map/ppermute | solution.py:264
  73.5 7.9 %collective-permute-start.11 = (bf16[64,2048]{1,0:T(8,128)(2,1)S(1)}, bf16[64,2048]{1,0:T(8,128)(2,1)S(1)}, u32[]{:S(2)}, u32[]{:S(2)}) collective-permute-start(bf16[64,2048]{1,0:T(8,128)(2,1)S(1)} %collective-permute-done.10.refs_4_), channel_id=1, source_target_pairs={{0,128},{224,96},{1,129},{225,97},{2,130},{226,98},{3,131},{227,99... | collective-permute-start | bytes 786440 | tf_op jit(solution)/shard_map/ppermute | solution.py:266
  81.4 12.8 %collective-permute-done.11.refs_5_ = bf16[64,2048]{1,0:T(8,128)(2,1)S(1)} collective-permute-done((bf16[64,2048]{1,0:T(8,128)(2,1)S(1)}, bf16[64,2048]{1,0:T(8,128)(2,1)S(1)}, u32[]{:S(2)}, u32[]{:S(2)}) %collective-permute-start.11) | collective-permute-done | bytes 262176 | tf_op jit(solution)/shard_map/ppermute | solution.py:266
  94.8 1.9 %collective-permute-start.13 = (bf16[2,192,512]{2,1,0:T(8,128)(2,1)S(1)}, bf16[2,192,512]{2,1,0:T(8,128)(2,1)S(1)}, u32[]{:S(2)}, u32[]{:S(2)}) collective-permute-start(bf16[2,192,512]{2,1,0:T(8,128)(2,1)S(1)} %get-tuple-element.37), channel_id=1, source_target_pairs={{1,2},{2,1},{3,4},{4,3},{5,6},{6,5},{7,8},{8,7},{9,10},{10,9},{11,... | collective-permute-start | bytes 1179656 | tf_op jit(solution)/shard_map/ppermute | solution.py:244
  96.7 2.7 %body.6.refs_2_ = f32[2,384,1024]{2,1,0:T(8,128)S(1)} custom-call(bf16[192,2048]{1,0:T(8,128)(2,1)S(1)} %collective-permute-done.8.refs_0_, bf16[128,2048]{1,0:T(8,128)(2,1)S(1)} %get-tuple-element.34.refs_1_, bf16[64,2048]{1,0:T(8,128)(2,1)S(1)} %get-tuple-element.35.refs_2_, bf16[128,2048]{1,0:T(8,128)(2,1)S(1)} %collective-permute-done.9.refs_3_, ...), custom_call_target="tpu_custom_call" | custom-call | flops 10000000000 | bytes 1 | tf_op jit(solution)/shard_map/body/pallas_call | solution.py:44
  99.4 6.6 %collective-permute-done.13.refs_1_ = bf16[2,192,512]{2,1,0:T(8,128)(2,1)S(1)} collective-permute-done((bf16[2,192,512]{2,1,0:T(8,128)(2,1)S(1)}, bf16[2,192,512]{2,1,0:T(8,128)(2,1)S(1)}, u32[]{:S(2)}, u32[]{:S(2)}) %collective-permute-start.13) | collective-permute-done | bytes 393248 | tf_op jit(solution)/shard_map/ppermute | solution.py:244
  106.0 1.1 edges.6
  108.3 7.0 %collective-permute-done.16.refs_4_ = bf16[64,2048]{1,0:T(8,128)(2,1)S(1)} collective-permute-done((bf16[64,2048]{1,0:T(8,128)(2,1)S(1)}, bf16[64,2048]{1,0:T(8,128)(2,1)S(1)}, u32[]{:S(2)}, u32[]{:S(2)}) %collective-permute-start.16) | collective-permute-done | bytes 262176 | tf_op jit(solution)/shard_map/ppermute | solution.py:264
  115.3 7.9 %collective-permute-start.17 = (bf16[64,2048]{1,0:T(8,128)(2,1)S(1)}, bf16[64,2048]{1,0:T(8,128)(2,1)S(1)}, u32[]{:S(2)}, u32[]{:S(2)}) collective-permute-start(bf16[64,2048]{1,0:T(8,128)(2,1)S(1)} %collective-permute-done.16.refs_4_), channel_id=1, source_target_pairs={{0,128},{224,96},{1,129},{225,97},{2,130},{226,98},{3,131},{227,99... | collective-permute-start | bytes 786440 | tf_op jit(solution)/shard_map/ppermute | solution.py:266
  123.2 16.1 %collective-permute-done.17.refs_5_ = bf16[64,2048]{1,0:T(8,128)(2,1)S(1)} collective-permute-done((bf16[64,2048]{1,0:T(8,128)(2,1)S(1)}, bf16[64,2048]{1,0:T(8,128)(2,1)S(1)}, u32[]{:S(2)}, u32[]{:S(2)}) %collective-permute-start.17) | collective-permute-done | bytes 262176 | tf_op jit(solution)/shard_map/ppermute | solution.py:266
  140.0 1.9 %collective-permute-start.19 = (bf16[2,192,512]{2,1,0:T(8,128)(2,1)S(1)}, bf16[2,192,512]{2,1,0:T(8,128)(2,1)S(1)}, u32[]{:S(2)}, u32[]{:S(2)}) collective-permute-start(bf16[2,192,512]{2,1,0:T(8,128)(2,1)S(1)} %get-tuple-element.42), channel_id=1, source_target_pairs={{1,2},{2,1},{3,4},{4,3},{5,6},{6,5},{7,8},{8,7},{9,10},{10,9},{11,... | collective-permute-start | bytes 1179656 | tf_op jit(solution)/shard_map/ppermute | solution.py:244
  141.9 2.7 %body.7.refs_2_ = f32[2,384,1024]{2,1,0:T(8,128)S(1)} custom-call(bf16[192,2048]{1,0:T(8,128)(2,1)S(1)} %collective-permute-done.14.refs_0_, bf16[128,2048]{1,0:T(8,128)(2,1)S(1)} %get-tuple-element.39.refs_1_, bf16[64,2048]{1,0:T(8,128)(2,1)S(1)} %get-tuple-element.40.refs_2_, bf16[128,2048]{1,0:T(8,128)(2,1)S(1)} %collective-permute-done.15.refs_3_, ...), custom_call_target="tpu_custom_call" | custom-call | flops 10000000000 | bytes 1 | tf_op jit(solution)/shard_map/body/pallas_call | solution.py:44
  144.6 6.6 %collective-permute-done.19.refs_1_ = bf16[2,192,512]{2,1,0:T(8,128)(2,1)S(1)} collective-permute-done((bf16[2,192,512]{2,1,0:T(8,128)(2,1)S(1)}, bf16[2,192,512]{2,1,0:T(8,128)(2,1)S(1)}, u32[]{:S(2)}, u32[]{:S(2)}) %collective-permute-start.19) | collective-permute-done | bytes 393248 | tf_op jit(solution)/shard_map/ppermute | solution.py:244
  151.2 1.1 edges.7
  153.2 8.7 %collective-permute-done.22.refs_4_ = bf16[80,2048]{1,0:T(8,128)(2,1)S(1)} collective-permute-done((bf16[80,2048]{1,0:T(8,128)(2,1)S(1)}, bf16[80,2048]{1,0:T(8,128)(2,1)S(1)}, u32[]{:S(2)}, u32[]{:S(2)}) %collective-permute-start.22) | collective-permute-done | bytes 327712 | tf_op jit(solution)/shard_map/ppermute | solution.py:264
  161.9 18.0 %collective-permute-start.23 = (bf16[80,2048]{1,0:T(8,128)(2,1)S(1)}, bf16[80,2048]{1,0:T(8,128)(2,1)S(1)}, u32[]{:S(2)}, u32[]{:S(2)}) collective-permute-start(bf16[80,2048]{1,0:T(8,128)(2,1)S(1)} %collective-permute-done.22.refs_4_), channel_id=1, source_target_pairs={{0,128},{224,96},{1,129},{225,97},{2,130},{226,98},{3,131},{227,99... | collective-permute-start | bytes 983048 | tf_op jit(solution)/shard_map/ppermute | solution.py:266
  179.9 5.4 %collective-permute-done.23.refs_5_ = bf16[80,2048]{1,0:T(8,128)(2,1)S(1)} collective-permute-done((bf16[80,2048]{1,0:T(8,128)(2,1)S(1)}, bf16[80,2048]{1,0:T(8,128)(2,1)S(1)}, u32[]{:S(2)}, u32[]{:S(2)}) %collective-permute-start.23) | collective-permute-done | bytes 327712 | tf_op jit(solution)/shard_map/ppermute | solution.py:266
  185.3 1.3 finish.1
  (35 shorter events, 6.6 us)
Async XLA Ops:
  0.6 6.1 %copy-start.2 = (f32[1,2048]{1,0:T(1,128)S(1)}, f32[1,2048]{1,0:T(1,128)}, u32[]{:S(2)}) copy-start(f32[1,2048]{1,0:T(1,128)} %refs_6_.11) | copy-start | bytes 24580
  0.6 6.1 %copy-start.1 = (bf16[1,192,2048]{2,1,0:T(8,128)(2,1)S(1)}, bf16[1,192,2048]{2,1,0:T(8,128)(2,1)}, u32[]{:S(2)}) copy-start(bf16[1,192,2048]{2,1,0:T(8,128)(2,1)} %refs_1_.3) | copy-start | bytes 2359300
  0.6 6.1 %copy-start = (bf16[1,192,2048]{2,1,0:T(8,128)(2,1)S(1)}, bf16[1,192,2048]{2,1,0:T(8,128)(2,1)}, u32[]{:S(2)}) copy-start(bf16[1,192,2048]{2,1,0:T(8,128)(2,1)} %refs_0_.3) | copy-start | bytes 2359300
  2.6 9.3 %collective-permute-start = (bf16[2,192,512]{2,1,0:T(8,128)(2,1)S(1)}, bf16[2,192,512]{2,1,0:T(8,128)(2,1)S(1)}, u32[]{:S(2)}, u32[]{:S(2)}) collective-permute-start(bf16[2,192,512]{2,1,0:T(8,128)(2,1)S(1)} %get-tuple-element.24), channel_id=1, source_target_pairs={{0,1},{1,0},{2,3},{3,2},{4,5},{5,4},{6,7},{7,6},{8,9},{9,8},{10,11... | collective-permute-start | bytes 1179656 | tf_op jit(solution)/shard_map/ppermute | solution.py:245
  3.4 11.2 %collective-permute-start.1 = (bf16[2,192,512]{2,1,0:T(8,128)(2,1)S(1)}, bf16[2,192,512]{2,1,0:T(8,128)(2,1)S(1)}, u32[]{:S(2)}, u32[]{:S(2)}) collective-permute-start(bf16[2,192,512]{2,1,0:T(8,128)(2,1)S(1)} %get-tuple-element.25), channel_id=1, source_target_pairs={{1,2},{2,1},{3,4},{4,3},{5,6},{6,5},{7,8},{8,7},{9,10},{10,9},{11,... | collective-permute-start | bytes 1179656 | tf_op jit(solution)/shard_map/ppermute | solution.py:244
  15.6 36.6 %collective-permute-start.2 = (bf16[192,2048]{1,0:T(8,128)(2,1)S(1)}, bf16[192,2048]{1,0:T(8,128)(2,1)S(1)}, u32[]{:S(2)}, u32[]{:S(2)}) collective-permute-start(bf16[192,2048]{1,0:T(8,128)(2,1)S(1)} %get-tuple-element.28), channel_id=1, source_target_pairs={{0,32},{32,0},{64,96},{96,64},{128,160},{160,128},{192,224},{224,1... | collective-permute-start | bytes 2359304 | tf_op jit(solution)/shard_map/ppermute | solution.py:263
  17.0 9.3 %collective-permute-start.4 = (bf16[80,2048]{1,0:T(8,128)(2,1)S(1)}, bf16[80,2048]{1,0:T(8,128)(2,1)S(1)}, u32[]{:S(2)}, u32[]{:S(2)}) collective-permute-start(bf16[80,2048]{1,0:T(8,128)(2,1)S(1)} %get-tuple-element.30.refs_2_), channel_id=1, source_target_pairs={{32,64},{64,32},{160,192},{192,160},{0,96},{96,0},{128,224},{224,1... | collective-permute-start | bytes 983048 | tf_op jit(solution)/shard_map/ppermute | solution.py:264
  18.9 16.2 %collective-permute-start.3 = (bf16[112,2048]{1,0:T(8,128)(2,1)S(1)}, bf16[112,2048]{1,0:T(8,128)(2,1)S(1)}, u32[]{:S(2)}, u32[]{:S(2)}) collective-permute-start(bf16[112,2048]{1,0:T(8,128)(2,1)S(1)} %get-tuple-element.29.refs_1_), channel_id=1, source_target_pairs={{32,64},{64,32},{160,192},{192,160},{96,128},{128,96},{33,65},{65,... | collective-permute-start | bytes 1376264 | tf_op jit(solution)/shard_map/ppermute | solution.py:265
  26.3 25.9 %collective-permute-start.5 = (bf16[80,2048]{1,0:T(8,128)(2,1)S(1)}, bf16[80,2048]{1,0:T(8,128)(2,1)S(1)}, u32[]{:S(2)}, u32[]{:S(2)}) collective-permute-start(bf16[80,2048]{1,0:T(8,128)(2,1)S(1)} %collective-permute-done.4.refs_4_), channel_id=1, source_target_pairs={{0,128},{224,96},{1,129},{225,97},{2,130},{226,98},{3,131},{227,99... | collective-permute-start | bytes 983048 | tf_op jit(solution)/shard_map/ppermute | solution.py:266
  52.7 4.8 %collective-permute-start.6 = (bf16[2,192,512]{2,1,0:T(8,128)(2,1)S(1)}, bf16[2,192,512]{2,1,0:T(8,128)(2,1)S(1)}, u32[]{:S(2)}, u32[]{:S(2)}) collective-permute-start(bf16[2,192,512]{2,1,0:T(8,128)(2,1)S(1)} %get-tuple-element.31), channel_id=1, source_target_pairs={{0,1},{1,0},{2,3},{3,2},{4,5},{5,4},{6,7},{7,6},{8,9},{9,8},{10,11... | collective-permute-start | bytes 1179656 | tf_op jit(solution)/shard_map/ppermute | solution.py:245
  52.9 11.2 %collective-permute-start.7 = (bf16[2,192,512]{2,1,0:T(8,128)(2,1)S(1)}, bf16[2,192,512]{2,1,0:T(8,128)(2,1)S(1)}, u32[]{:S(2)}, u32[]{:S(2)}) collective-permute-start(bf16[2,192,512]{2,1,0:T(8,128)(2,1)S(1)} %get-tuple-element.32), channel_id=1, source_target_pairs={{1,2},{2,1},{3,4},{4,3},{5,6},{6,5},{7,8},{8,7},{9,10},{10,9},{11,... | collective-permute-start | bytes 1179656 | tf_op jit(solution)/shard_map/ppermute | solution.py:244
  65.2 29.0 %collective-permute-start.8 = (bf16[192,2048]{1,0:T(8,128)(2,1)S(1)}, bf16[192,2048]{1,0:T(8,128)(2,1)S(1)}, u32[]{:S(2)}, u32[]{:S(2)}) collective-permute-start(bf16[192,2048]{1,0:T(8,128)(2,1)S(1)} %get-tuple-element.33), channel_id=1, source_target_pairs={{0,32},{32,0},{64,96},{96,64},{128,160},{160,128},{192,224},{224,1... | collective-permute-start | bytes 2359304 | tf_op jit(solution)/shard_map/ppermute | solution.py:263
  65.3 8.2 %collective-permute-start.10 = (bf16[64,2048]{1,0:T(8,128)(2,1)S(1)}, bf16[64,2048]{1,0:T(8,128)(2,1)S(1)}, u32[]{:S(2)}, u32[]{:S(2)}) collective-permute-start(bf16[64,2048]{1,0:T(8,128)(2,1)S(1)} %get-tuple-element.35.refs_2_), channel_id=1, source_target_pairs={{32,64},{64,32},{160,192},{192,160},{0,96},{96,0},{128,224},{224,1... | collective-permute-start | bytes 786440 | tf_op jit(solution)/shard_map/ppermute | solution.py:264
  65.6 28.7 %collective-permute-start.9 = (bf16[128,2048]{1,0:T(8,128)(2,1)S(1)}, bf16[128,2048]{1,0:T(8,128)(2,1)S(1)}, u32[]{:S(2)}, u32[]{:S(2)}) collective-permute-start(bf16[128,2048]{1,0:T(8,128)(2,1)S(1)} %get-tuple-element.34.refs_1_), channel_id=1, source_target_pairs={{32,64},{64,32},{160,192},{192,160},{96,128},{128,96},{33,65},{65,... | collective-permute-start | bytes 1572872 | tf_op jit(solution)/shard_map/ppermute | solution.py:265
  73.5 20.7 %collective-permute-start.11 = (bf16[64,2048]{1,0:T(8,128)(2,1)S(1)}, bf16[64,2048]{1,0:T(8,128)(2,1)S(1)}, u32[]{:S(2)}, u32[]{:S(2)}) collective-permute-start(bf16[64,2048]{1,0:T(8,128)(2,1)S(1)} %collective-permute-done.10.refs_4_), channel_id=1, source_target_pairs={{0,128},{224,96},{1,129},{225,97},{2,130},{226,98},{3,131},{227,99... | collective-permute-start | bytes 786440 | tf_op jit(solution)/shard_map/ppermute | solution.py:266
  94.7 4.7 %collective-permute-start.12 = (bf16[2,192,512]{2,1,0:T(8,128)(2,1)S(1)}, bf16[2,192,512]{2,1,0:T(8,128)(2,1)S(1)}, u32[]{:S(2)}, u32[]{:S(2)}) collective-permute-start(bf16[2,192,512]{2,1,0:T(8,128)(2,1)S(1)} %get-tuple-element.36), channel_id=1, source_target_pairs={{0,1},{1,0},{2,3},{3,2},{4,5},{5,4},{6,7},{7,6},{8,9},{9,8},{10,11... | collective-permute-start | bytes 1179656 | tf_op jit(solution)/shard_map/ppermute | solution.py:245
  94.8 11.2 %collective-permute-start.13 = (bf16[2,192,512]{2,1,0:T(8,128)(2,1)S(1)}, bf16[2,192,512]{2,1,0:T(8,128)(2,1)S(1)}, u32[]{:S(2)}, u32[]{:S(2)}) collective-permute-start(bf16[2,192,512]{2,1,0:T(8,128)(2,1)S(1)} %get-tuple-element.37), channel_id=1, source_target_pairs={{1,2},{2,1},{3,4},{4,3},{5,6},{6,5},{7,8},{8,7},{9,10},{10,9},{11,... | collective-permute-start | bytes 1179656 | tf_op jit(solution)/shard_map/ppermute | solution.py:244
  107.1 32.3 %collective-permute-start.14 = (bf16[192,2048]{1,0:T(8,128)(2,1)S(1)}, bf16[192,2048]{1,0:T(8,128)(2,1)S(1)}, u32[]{:S(2)}, u32[]{:S(2)}) collective-permute-start(bf16[192,2048]{1,0:T(8,128)(2,1)S(1)} %get-tuple-element.38), channel_id=1, source_target_pairs={{0,32},{32,0},{64,96},{96,64},{128,160},{160,128},{192,224},{224,1... | collective-permute-start | bytes 2359304 | tf_op jit(solution)/shard_map/ppermute | solution.py:263
  107.2 8.2 %collective-permute-start.16 = (bf16[64,2048]{1,0:T(8,128)(2,1)S(1)}, bf16[64,2048]{1,0:T(8,128)(2,1)S(1)}, u32[]{:S(2)}, u32[]{:S(2)}) collective-permute-start(bf16[64,2048]{1,0:T(8,128)(2,1)S(1)} %get-tuple-element.40.refs_2_), channel_id=1, source_target_pairs={{32,64},{64,32},{160,192},{192,160},{0,96},{96,0},{128,224},{224,1... | collective-permute-start | bytes 786440 | tf_op jit(solution)/shard_map/ppermute | solution.py:264
  107.6 31.7 %collective-permute-start.15 = (bf16[128,2048]{1,0:T(8,128)(2,1)S(1)}, bf16[128,2048]{1,0:T(8,128)(2,1)S(1)}, u32[]{:S(2)}, u32[]{:S(2)}) collective-permute-start(bf16[128,2048]{1,0:T(8,128)(2,1)S(1)} %get-tuple-element.39.refs_1_), channel_id=1, source_target_pairs={{32,64},{64,32},{160,192},{192,160},{96,128},{128,96},{33,65},{65,... | collective-permute-start | bytes 1572872 | tf_op jit(solution)/shard_map/ppermute | solution.py:265
  115.3 24.0 %collective-permute-start.17 = (bf16[64,2048]{1,0:T(8,128)(2,1)S(1)}, bf16[64,2048]{1,0:T(8,128)(2,1)S(1)}, u32[]{:S(2)}, u32[]{:S(2)}) collective-permute-start(bf16[64,2048]{1,0:T(8,128)(2,1)S(1)} %collective-permute-done.16.refs_4_), channel_id=1, source_target_pairs={{0,128},{224,96},{1,129},{225,97},{2,130},{226,98},{3,131},{227,99... | collective-permute-start | bytes 786440 | tf_op jit(solution)/shard_map/ppermute | solution.py:266
  139.8 4.8 %collective-permute-start.18 = (bf16[2,192,512]{2,1,0:T(8,128)(2,1)S(1)}, bf16[2,192,512]{2,1,0:T(8,128)(2,1)S(1)}, u32[]{:S(2)}, u32[]{:S(2)}) collective-permute-start(bf16[2,192,512]{2,1,0:T(8,128)(2,1)S(1)} %get-tuple-element.41), channel_id=1, source_target_pairs={{0,1},{1,0},{2,3},{3,2},{4,5},{5,4},{6,7},{7,6},{8,9},{9,8},{10,11... | collective-permute-start | bytes 1179656 | tf_op jit(solution)/shard_map/ppermute | solution.py:245
  140.0 11.2 %collective-permute-start.19 = (bf16[2,192,512]{2,1,0:T(8,128)(2,1)S(1)}, bf16[2,192,512]{2,1,0:T(8,128)(2,1)S(1)}, u32[]{:S(2)}, u32[]{:S(2)}) collective-permute-start(bf16[2,192,512]{2,1,0:T(8,128)(2,1)S(1)} %get-tuple-element.42), channel_id=1, source_target_pairs={{1,2},{2,1},{3,4},{4,3},{5,6},{6,5},{7,8},{8,7},{9,10},{10,9},{11,... | collective-permute-start | bytes 1179656 | tf_op jit(solution)/shard_map/ppermute | solution.py:244
  152.3 33.0 %collective-permute-start.20 = (bf16[192,2048]{1,0:T(8,128)(2,1)S(1)}, bf16[192,2048]{1,0:T(8,128)(2,1)S(1)}, u32[]{:S(2)}, u32[]{:S(2)}) collective-permute-start(bf16[192,2048]{1,0:T(8,128)(2,1)S(1)} %get-tuple-element.43), channel_id=1, source_target_pairs={{0,32},{32,0},{64,96},{96,64},{128,160},{160,128},{192,224},{224,1... | collective-permute-start | bytes 2359304 | tf_op jit(solution)/shard_map/ppermute | solution.py:263
  152.4 9.5 %collective-permute-start.22 = (bf16[80,2048]{1,0:T(8,128)(2,1)S(1)}, bf16[80,2048]{1,0:T(8,128)(2,1)S(1)}, u32[]{:S(2)}, u32[]{:S(2)}) collective-permute-start(bf16[80,2048]{1,0:T(8,128)(2,1)S(1)} %get-tuple-element.45.refs_2_), channel_id=1, source_target_pairs={{32,64},{64,32},{160,192},{192,160},{0,96},{96,0},{128,224},{224,1... | collective-permute-start | bytes 983048 | tf_op jit(solution)/shard_map/ppermute | solution.py:264
  152.5 27.4 %collective-permute-start.21 = (bf16[112,2048]{1,0:T(8,128)(2,1)S(1)}, bf16[112,2048]{1,0:T(8,128)(2,1)S(1)}, u32[]{:S(2)}, u32[]{:S(2)}) collective-permute-start(bf16[112,2048]{1,0:T(8,128)(2,1)S(1)} %get-tuple-element.44.refs_1_), channel_id=1, source_target_pairs={{32,64},{64,32},{160,192},{192,160},{96,128},{128,96},{33,65},{65,... | collective-permute-start | bytes 1376264 | tf_op jit(solution)/shard_map/ppermute | solution.py:265
  161.9 23.5 %collective-permute-start.23 = (bf16[80,2048]{1,0:T(8,128)(2,1)S(1)}, bf16[80,2048]{1,0:T(8,128)(2,1)S(1)}, u32[]{:S(2)}, u32[]{:S(2)}) collective-permute-start(bf16[80,2048]{1,0:T(8,128)(2,1)S(1)} %collective-permute-done.22.refs_4_), channel_id=1, source_target_pairs={{0,128},{224,96},{1,129},{225,97},{2,130},{226,98},{3,131},{227,99... | collective-permute-start | bytes 983048 | tf_op jit(solution)/shard_map/ppermute | solution.py:266
